TPU v7x, 512 devices: a whole 4x8x8 slice. The times are simulated.
512 devices in a mesh: seq: 64 (over z, y), head: 8 (over x, core).
Axes of the slice: x: 4, y: 8, z: 8, core: 2. Of those that a mesh axis runs over, the one named last changes fastest.
Arguments:
- queries: bfloat16 [9216, 8192], P('seq', 'head'), may hold values from -24 to 24
- key_matrix: bfloat16 [9216, 1024], P('seq', 'head'), may hold values from -4 to 4
- value_matrix: bfloat16 [9216, 1024], P('seq', 'head'), may hold values from -6 to 6
- query_feature_weight: bfloat16 [128, 4096], P(None, 'head'), may hold values from -0.5 to 0.5
- key_feature_weight: bfloat16 [128, 512], P(None, 'head'), may hold values from -0.5 to 0.5
Outputs:
- student_out: bfloat16 [9216, 8192], P('seq', 'head')
- query_map_grad: float32 [128, 4096], P(None, 'head')
- key_weight_gradient: float32 [128, 512], P(None, 'head')
- transfer_loss: float32 [], replicated
All inputs are finite; a program needn't handle non-finite values.
Results may differ from a plain program's by a relative error of at most 0.008.
Values may be sent and summed in bfloat16 or wider, within the bound.
A program may use at most 128 MiB of HBM per device.

v0:
```python
import jax
import jax.numpy as jnp
from jax import lax
from jax.sharding import PartitionSpec as P

HEAD_SIZE = 128
GROUP_QUERIES = 8
HALF_FEATURES = 64


NEG_LARGE = -1e30


def prefix(shard, axis, join, neutral, backward):
    count = lax.axis_size(axis)
    place = lax.axis_index(axis)
    ahead = count - 1 - place if backward else place
    gathered = jax.tree.map(
        lambda a, kind: lax.all_gather(a.astype(kind), axis), shard, (jnp.bfloat16, jnp.bfloat16)
    )
    state = jax.tree.map(lambda a, e: jnp.zeros_like(a) + jnp.asarray(e, a.dtype), shard, neutral)

    def one(lap, state):
        source = count - 1 - lap if backward else lap
        return join(
            state,
            jax.tree.map(
                lambda a, own: lax.dynamic_index_in_dim(a, source, 0, False).astype(own.dtype),
                gathered,
                shard,
            ),
        )

    return lax.fori_loop(0, ahead, one, state)


def feature_pair(logits):
    plus_half = jax.nn.softmax(logits, axis=-1)
    minus_half = jax.nn.softmax(-logits, axis=-1)
    return (plus_half, minus_half)


def pair_backward(plus_half, minus_half, d_features):
    feat_count = plus_half.shape[-1]
    d_plus = d_features[..., :feat_count]
    d_minus = d_features[..., feat_count:]
    inner_plus = jnp.sum(d_plus * plus_half, axis=-1, keepdims=True)
    inner_minus = jnp.sum(d_minus * minus_half, axis=-1, keepdims=True)
    return plus_half * (d_plus - inner_plus) - minus_half * (d_minus - inner_minus)


def add_pair(earlier_pair, later_pair):
    return (earlier_pair[0] + later_pair[0], earlier_pair[1] + later_pair[1])


def attend(running, row_block, query_pos, key_view, value_view, key_pos, score_scale):
    row_max, row_sum, weighted = running
    scores = (
        jnp.einsum("rkgd,lkd->kgrl", row_block, key_view, preferred_element_type=jnp.float32)
        * score_scale
    )
    visible = key_pos[None, None, None, :] <= query_pos[None, None, :, None]
    masked = jnp.where(visible, scores, NEG_LARGE)
    new_max = jnp.maximum(row_max, jnp.max(masked, axis=-1))
    exponent = jnp.where(visible, jnp.exp(masked - new_max[..., None]), 0.0)
    weights = exponent.astype(jnp.bfloat16)
    weighted = jnp.einsum("kgrl,lkd->kgrd", weights, value_view, preferred_element_type=jnp.float32)
    row_sum = jnp.sum(exponent, axis=-1)
    return (new_max, row_sum, weighted)


def local(queries, key_matrix, value_matrix, query_feature_weight, key_feature_weight):
    token_rows = queries.shape[0]
    local_heads = key_matrix.shape[1] // HEAD_SIZE
    seq_count = lax.axis_size("seq")
    position = lax.axis_index("seq")
    first_row = position * token_rows
    seg_total = token_rows * seq_count
    score_scale = HEAD_SIZE ** (-0.5)
    query_heads = queries.reshape(token_rows, local_heads, GROUP_QUERIES, HEAD_SIZE)
    key_heads = key_matrix.reshape(token_rows, local_heads, HEAD_SIZE)
    value_heads = value_matrix.reshape(token_rows, local_heads, HEAD_SIZE)
    query_map_view = query_feature_weight.reshape(
        HEAD_SIZE, local_heads, GROUP_QUERIES, HALF_FEATURES
    )
    key_map_view = key_feature_weight.reshape(HEAD_SIZE, local_heads, HALF_FEATURES)
    query_sets = ((query_heads, first_row + jnp.arange(token_rows, dtype=jnp.int32)),)

    def fresh_carry(row_block):
        row_count = row_block.shape[0]
        return (
            jnp.full((local_heads, GROUP_QUERIES, row_count), NEG_LARGE, jnp.float32),
            jnp.zeros((local_heads, GROUP_QUERIES, row_count), jnp.float32),
            jnp.zeros((local_heads, GROUP_QUERIES, row_count, HEAD_SIZE), jnp.float32),
        )

    first_key = jnp.int32(0)
    key_block = lax.all_gather(key_matrix, "seq", axis=0, tiled=True)
    value_block = lax.all_gather(value_matrix, "seq", axis=0, tiled=True)
    key_count = key_block.shape[0]
    key_view = key_block.reshape(key_count, local_heads, HEAD_SIZE)
    value_view = value_block.reshape(key_count, local_heads, HEAD_SIZE)
    key_pos = jnp.arange(key_count, dtype=jnp.int32)
    teach_runs = tuple((fresh_carry(query_set[0]) for query_set in query_sets))
    updated = []
    for query_set, fold_teach_run in zip(query_sets, teach_runs):
        row_block, query_pos = query_set

        def visit_block(current, row_block=row_block, query_pos=query_pos):
            return attend(current, row_block, query_pos, key_view, value_view, key_pos, score_scale)

        def unchanged(current):
            return current

        updated.append(lax.cond(first_key <= query_pos[-1], visit_block, unchanged, fold_teach_run))
    teach_done = tuple(updated)

    def finish(teach_run):
        return (teach_run[2] / teach_run[1][..., None]).astype(jnp.bfloat16)

    finished = [finish(teach_run) for teach_run in teach_done]
    teacher = finished[0]
    query_logits = jnp.einsum(
        "tkgd,dkgf->kgtf", query_heads, query_map_view, preferred_element_type=jnp.float32
    )
    query_plus, query_minus = feature_pair(query_logits)
    query_phi = jnp.concatenate([query_plus, query_minus], axis=-1).astype(jnp.bfloat16)
    logits = jnp.einsum("lkd,dkf->klf", key_heads, key_map_view, preferred_element_type=jnp.float32)
    plus_half, minus_half = feature_pair(logits)
    key_phi = jnp.concatenate([plus_half, minus_half], axis=-1).astype(jnp.bfloat16)
    block_state = jnp.einsum(
        "ktf,tkd->kfd", key_phi, value_heads, preferred_element_type=jnp.float32
    )
    block_norm = jnp.sum(key_phi.astype(jnp.float32), axis=1)
    zero_pair = (jnp.zeros_like(block_state), jnp.zeros_like(block_norm))
    prefix_state, prefix_norm = prefix((block_state, block_norm), "seq", add_pair, zero_pair, False)
    prefix_low = prefix_state.astype(jnp.bfloat16)
    token_index = jnp.arange(token_rows, dtype=jnp.int32)
    causal = token_index[None, :] <= token_index[:, None]
    intra_scores = jnp.where(
        causal,
        jnp.einsum("kgtf,ksf->kgts", query_phi, key_phi, preferred_element_type=jnp.float32),
        0.0,
    )
    numerator = jnp.einsum(
        "kgts,skd->kgtd",
        intra_scores.astype(jnp.bfloat16),
        value_heads,
        preferred_element_type=jnp.float32,
    )
    numerator = numerator + jnp.einsum(
        "kgtf,kfd->kgtd", query_phi, prefix_low, preferred_element_type=jnp.float32
    )
    query_wide = query_phi.astype(jnp.float32)
    denominator = jnp.sum(intra_scores, axis=-1) + jnp.einsum(
        "kgtf,kf->kgt", query_wide, prefix_norm, precision=lax.Precision.HIGHEST
    )
    student = numerator / denominator[..., None]
    target = teacher.astype(jnp.float32)
    differ = student - target
    loss_local = jnp.sum(differ * differ)
    grad_out = 2.0 * differ / seg_total
    numer_grad = grad_out / denominator[..., None]
    denom_grad = -jnp.sum(grad_out * student, axis=-1) / denominator
    numer_low = numer_grad.astype(jnp.bfloat16)
    coupling = (
        jnp.einsum("kgtd,skd->kgts", numer_low, value_heads, preferred_element_type=jnp.float32)
        + denom_grad[..., None]
    )
    coupling_low = jnp.where(causal, coupling, 0.0).astype(jnp.bfloat16)
    later_state = jnp.einsum(
        "kgtf,kgtd->kfd", query_phi, numer_low, preferred_element_type=jnp.float32
    )
    later_norm = jnp.einsum("kgtf,kgt->kf", query_wide, denom_grad, precision=lax.Precision.HIGHEST)
    zero_later = (jnp.zeros_like(later_state), jnp.zeros_like(later_norm))
    suffix_state, suffix_norm = prefix((later_state, later_norm), "seq", add_pair, zero_later, True)
    suffix_low = suffix_state.astype(jnp.bfloat16)
    query_dphi = jnp.einsum(
        "kgts,ksf->kgtf", coupling_low, key_phi, preferred_element_type=jnp.float32
    )
    query_dphi = query_dphi + jnp.einsum(
        "kgtd,kfd->kgtf", numer_low, prefix_low, preferred_element_type=jnp.float32
    )
    query_dphi = query_dphi + denom_grad[..., None] * prefix_norm[:, None, None, :]
    key_dphi = jnp.einsum(
        "kgts,kgtf->ksf", coupling_low, query_phi, preferred_element_type=jnp.float32
    )
    key_dphi = key_dphi + jnp.einsum(
        "skd,kfd->ksf", value_heads, suffix_low, preferred_element_type=jnp.float32
    )
    key_dphi = key_dphi + suffix_norm[:, None, :]
    query_dlogit = pair_backward(query_plus, query_minus, query_dphi).astype(jnp.bfloat16)
    key_dlogit = pair_backward(plus_half, minus_half, key_dphi).astype(jnp.bfloat16)
    query_grad = jnp.einsum(
        "tkgd,kgtf->dkgf", query_heads, query_dlogit, preferred_element_type=jnp.float32
    )
    key_grad = jnp.einsum("tkd,ktf->dkf", key_heads, key_dlogit, preferred_element_type=jnp.float32)
    query_grad, key_grad = lax.psum((query_grad, key_grad), "seq")
    transfer_loss = lax.psum(loss_local, ("seq", "head")) / seg_total
    student_out = (
        student.astype(jnp.bfloat16)
        .transpose(2, 0, 1, 3)
        .reshape(token_rows, local_heads * GROUP_QUERIES * HEAD_SIZE)
    )
    return (
        student_out,
        query_grad.reshape(HEAD_SIZE, local_heads * GROUP_QUERIES * HALF_FEATURES),
        key_grad.reshape(HEAD_SIZE, local_heads * HALF_FEATURES),
        transfer_loss,
    )


def solution(mesh):
    placed = (
        P("seq", "head"),
        P("seq", "head"),
        P("seq", "head"),
        P(None, "head"),
        P(None, "head"),
    )
    return jax.shard_map(
        local,
        mesh=mesh,
        in_specs=placed,
        out_specs=(P("seq", "head"), P(None, "head"), P(None, "head"), P()),
        check_vma=False,
    )
```

profile of v0, /device:TPU:2, one launch (start us, length us, event | category | flops | bytes accessed | tf_op | source)
XLA Modules:
  0.0 812.8 jit_solution(13775298181172924217)
XLA Ops:
  7.9 0.9 fusion.99
  8.9 1.5 convolution_convert_fusion
  13.4 1.0 copy.51
  14.5 49.8 %all-gather.4 = bf16[64,1,128]{2,1,0:T(2,128)(2,1)S(1)} all-gather(bf16[1,1,128]{2,1,0:T(2,128)(2,1)S(1)} %bitcast.271), channel_id=3, replica_groups=mesh['seq'=64,'head'=8] {'seq'}, dimensions={0}, use_global_device_ids=true | all-gather | bytes 16640 | tf_op jit(solution)/shard_map/all_gather | solution.py:19
  64.3 1.3 fusion.103
  65.7 1.3 fusion.100
  67.5 1.1 fusion.38
  68.7 31.2 %all-gather.15.cloned.1.call-done = bf16[8192,128]{1,0:T(8,128)(2,1)} async-done(((bf16[128,128]{1,0:T(8,128)(2,1)}), bf16[8192,128]{1,0:T(8,128)(2,1)}) %all-gather.15.cloned.1.call-update) | async-done | bytes 2097168 | tf_op jit(solution)/shard_map/all_gather | solution.py:19
  100.2 83.5 %all-gather.11.cloned.1.call-done = bf16[9216,128]{1,0:T(8,128)(2,1)} async-done(((bf16[144,128]{1,0:T(8,128)(2,1)}), bf16[9216,128]{1,0:T(8,128)(2,1)}) %all-gather.11.cloned.1.call-update) | async-done | bytes 2359312 | tf_op jit(solution)/shard_map/all_gather | solution.py:98
  183.7 83.7 %all-gather.13.cloned.1.call-done = bf16[9216,128]{1,0:T(8,128)(2,1)} async-done(((bf16[144,128]{1,0:T(8,128)(2,1)}), bf16[9216,128]{1,0:T(8,128)(2,1)}) %all-gather.13.cloned.1.call-update) | async-done | bytes 2359312 | tf_op jit(solution)/shard_map/all_gather | solution.py:99
  267.4 62.5 %conditional.1 = (f32[1,8,144]{2,1,0:T(8,128)}, f32[1,8,144,128]{3,2,1,0:T(8,128)}) conditional(s32[]{:T(128)} %bitcast.28, () %tuple.33, (s32[9216]{0:T(1024)S(1)}, s32[144]{0:T(256)}, bf16[144,1024]{1,0:T(8,128)(2,1)}, bf16[9216,128]{1,0:T(8,128)(2,1)}, bf16[9216,128]{1,0:T(8,128)(2,1)}) %tuple.98), branch_computations={%region_12.13_spmd, %region_13.16_spmd} | conditional | flops 5575162880 | bytes 138378832 | solution.py:115
  267.6 1.4 broadcast_compare_fusion
  269.0 18.7 %fusion = (f32[8,144]{1,0:T(8,128)S(1)}, f32[9216,144,8]{0,1,2:T(8,128)}) fusion(pred[144,9216]{1,0:T(8,128)(4,1)S(1)} %broadcast_compare_fusion, bf16[9216,128]{1,0:T(8,128)(2,1)} %get-tuple-element.118, bf16[144,1024]{1,0:T(8,128)(2,1)} %get-tuple-element.119), kind=kOutput, calls=%fused_computation.4 | convolution fusion | flops 2749758464 | bytes 46453248 | tf_op jit(solution)/shard_map/cond/branch_1_fun/rkgd,lkd->kgrl/dot_general | solution.py:59
  287.7 21.9 %fusion.2 = f32[8,144]{1,0:T(8,128)} fusion(f32[9216,144,8]{0,1,2:T(8,128)} %get-tuple-element.217, f32[8,144]{1,0:T(8,128)S(1)} %broadcast_maximum_fusion, pred[144,9216]{1,0:T(8,128)(4,1)S(1)} %broadcast_compare_fusion), kind=kLoop, calls=%fused_computation.6 | loop fusion | flops 53083008 | bytes 43803648 | tf_op jit(solution)/shard_map/cond/branch_1_fun/reduce_sum | solution.py:68
  309.6 20.2 %fusion.10 = f32[1,8,144,128]{3,2,1,0:T(8,128)} fusion(bf16[9216,128]{1,0:T(8,128)(2,1)} %get-tuple-element.120, f32[9216,144,8]{0,1,2:T(8,128)} %get-tuple-element.217, f32[8,144]{1,0:T(8,128)S(1)} %broadcast_maximum_fusion, pred[144,9216]{1,0:T(8,128)(4,1)S(1)} %broadcast_compare_fusion), kind=kOutput, calls=%fused_computation.14 | convolution fusion | flops 2770993152 | bytes 46748160 | tf_op jit(solution)/shard_map/cond/branch_1_fun/kgrl,lkd->kgrd/dot_general | solution.py:67
  329.9 2.8 multiply_reduce_fusion
  332.9 1.9 fusion.34
  334.9 95.5 %psum.23 = f32[]{:T(128)} all-reduce(f32[]{:T(128)} %get-tuple-element.183), channel_id=1, replica_groups=mesh['seq'=64,'head'=8] {'seq','head'}, use_global_device_ids=true, to_apply=%region_26.27 | all-reduce | flops 1 | bytes 8 | tf_op jit(solution)/shard_map/psum | solution.py:199
  432.8 0.8 copy.65
  434.1 42.6 %all-gather.5 = bf16[64,1,128]{2,1,0:T(2,128)(2,1)S(1)} all-gather(bf16[1,1,128]{2,1,0:T(2,128)(2,1)S(1)} %fusion.36), channel_id=5, replica_groups=mesh['seq'=64,'head'=8] {'seq'}, dimensions={0}, use_global_device_ids=true | all-gather | bytes 16640 | tf_op jit(solution)/shard_map/all_gather | solution.py:19
  477.8 51.3 %while.27 = (s32[]{:T(128)}, f32[1,128,128]{2,1,0:T(8,128)S(1)}, f32[1,128]{1,0:T(1,128)S(1)}, s32[]{:T(128)}, bf16[64,1,128,128]{3,2,1,0:T(8,128)(2,1)}, /*inde...) while((s32[]{:T(128)}, f32[1,128,128]{2,1,0:T(8,128)S(1)}, ...), condition=%wide.region_21.22_spmd, body=%wide.region_20.21_spmd.sunk | while | flops 33030 | bytes 165283 | solution.py:34
  478.6 0.8 convert_add_fusion.10
  480.2 0.8 convert_add_fusion.10
  481.9 0.8 convert_add_fusion.10
  483.5 0.8 convert_add_fusion.10
  484.3 0.8 convert_add_fusion.10
  490.0 0.8 convert_add_fusion.10
  490.8 0.8 convert_add_fusion.10
  492.5 0.8 convert_add_fusion.10
  494.1 0.8 convert_add_fusion.10
  494.9 0.8 convert_add_fusion.10
  495.7 0.8 convert_add_fusion.10
  497.3 0.8 convert_add_fusion.10
  498.2 0.8 convert_add_fusion.10
  499.0 0.8 convert_add_fusion.10
  501.4 0.8 convert_add_fusion.10
  502.2 0.8 convert_add_fusion.10
  503.9 0.8 convert_add_fusion.10
  504.7 0.8 convert_add_fusion.10
  505.5 0.8 convert_add_fusion.10
  507.9 0.8 convert_add_fusion.10
  508.8 0.8 convert_add_fusion.10
  509.6 0.8 convert_add_fusion.10
  511.2 0.8 convert_add_fusion.10
  512.0 0.8 convert_add_fusion.10
  519.3 0.8 convert_add_fusion.10
  529.5 274.0 %psum.22 = f32[128,64]{0,1:T(8,128)} all-reduce(f32[128,64]{0,1:T(8,128)S(1)} %convolution_bitcast_fusion.3), channel_id=1, replica_groups=mesh['seq'=64,'head'=8] {'seq'}, use_global_device_ids=true, to_apply=%region_24.25 | all-reduce | flops 8192 | bytes 65536 | tf_op jit(solution)/shard_map/psum | solution.py:198
  803.5 1.7 copy.144
  (171 shorter events, 38.2 us)
Async XLA Ops:
  7.2 0.7 copy-start
  7.2 92.6 %all-gather.15.cloned.1.call-start = ((), (), s32[]{:S(2)}) async-start(), calls=%async_computation.3 | async-start | bytes 2129920 | tf_op jit(solution)/shard_map/all_gather | solution.py:19
  8.8 4.5 copy-start.5
  8.9 4.4 copy-start.7
  8.9 4.4 copy-start.9
  10.5 173.1 %all-gather.11.cloned.1.call-start = ((), (), s32[]{:S(2)}) async-start(), calls=%async_computation | async-start | bytes 2396160 | tf_op jit(solution)/shard_map/all_gather | solution.py:98
  11.3 256.1 %all-gather.13.cloned.1.call-start = ((), (), s32[]{:S(2)}) async-start(), calls=%async_computation.1 | async-start | bytes 2396160 | tf_op jit(solution)/shard_map/all_gather | solution.py:99
  12.0 465.7 %all-gather.17.cloned.1.call-start = ((), (), s32[]{:S(2)}) async-start(), calls=%async_computation.4 | async-start | bytes 2129920 | tf_op jit(solution)/shard_map/all_gather | solution.py:19
  12.1 1.3 copy-start.11
  67.1 200.2 %copy-start.2 = (bf16[8,144,64]{1,2,0:T(8,128)(2,1)}, bf16[8,144,64]{1,2,0:T(8,128)(2,1)S(1)}, u32[]{:S(2)}) copy-start(bf16[8,144,64]{1,2,0:T(8,128)(2,1)S(1)} %get-tuple-element.233) | copy-start | bytes 442372
  267.4 163.9 %copy-start.1 = (bf16[144,128]{1,0:T(8,128)(2,1)S(1)}, bf16[144,128]{1,0:T(8,128)(2,1)}, u32[]{:S(2)}) copy-start(bf16[144,128]{1,0:T(8,128)(2,1)} %param.13) | copy-start | bytes 110596
  329.9 102.6 %copy-start.12 = (bf16[144,1024]{1,0:T(8,128)(2,1)S(1)}, bf16[144,1024]{1,0:T(8,128)(2,1)}, u32[]{:S(2)}) copy-start(bf16[144,1024]{1,0:T(8,128)(2,1)} %param.11) | copy-start | bytes 884740
  329.9 103.8 %copy-start.3 = (bf16[8,144,64]{1,2,0:T(8,128)(2,1)S(1)}, bf16[8,144,64]{1,2,0:T(8,128)(2,1)}, u32[]{:S(2)}) copy-start(bf16[8,144,64]{1,2,0:T(8,128)(2,1)} %copy-done.2) | copy-start | bytes 442372
  332.7 196.6 %copy-start.6 = (f32[144]{0:T(256)S(1)}, f32[144]{0:T(256)}, u32[]{:S(2)}) copy-start(f32[144]{0:T(256)} %copy-done.5) | copy-start | bytes 1732
  332.7 196.6 %copy-start.8 = (f32[144]{0:T(256)S(1)}, f32[144]{0:T(256)}, u32[]{:S(2)}) copy-start(f32[144]{0:T(256)} %copy-done.7) | copy-start | bytes 1732
  332.7 196.6 %copy-start.10 = (f32[144]{0:T(256)S(1)}, f32[144]{0:T(256)}, u32[]{:S(2)}) copy-start(f32[144]{0:T(256)} %copy-done.9) | copy-start | bytes 1732
  332.9 196.5 %copy-start.4 = (bf16[144,128]{1,0:T(8,128)(2,1)S(1)}, bf16[144,128]{1,0:T(8,128)(2,1)}, u32[]{:S(2)}) copy-start(bf16[144,128]{1,0:T(8,128)(2,1)} %param.12) | copy-start | bytes 110596
  334.8 468.7 %all-reduce.2.cloned.1.call-start = ((), (), s32[]{:S(2)}) async-start(), calls=%async_computation.2 | async-start | bytes 524288 | tf_op jit(solution)/shard_map/psum | solution.py:198
Sparse Core Ops, SparseCore 0:
  11.6 88.1 all-gather.14
  102.9 80.7 all-gather.10
  186.7 80.5 all-gather.12
  334.9 80.1 all-gather.16
  477.2 147.5 all-reduce.1
where the time goes:
time: 818 us; the launch traced here: 813 us
  blocking collectives  462 us (56%)
  waiting for transfers between devices  200 us (24%)
  other arithmetic  73.9 us (9%)
  matrix products  53 us (6%)
  between operations  16.5 us (2%)
    psum x1, blocking collectives, local(): query_grad, key_grad = lax.psum((query_grad, key_grad), 'seq')  274 us
    psum x1, blocking collectives, local(): transfer_loss = lax.psum(loss_local, ('seq', 'head')) / seg_total  95.5 us
    all_gather x2, blocking collectives, prefix(): lax.all_gather(a.astype(kind), axis)  92.4 us
    all_gather x1, waiting for transfers between devices, local(): value_block = lax.all_gather(value_matrix, 'seq', axis=0, tiled=True)  83.7 us
    all_gather x1, waiting for transfers between devices, local(): key_block = lax.all_gather(key_matrix, 'seq', axis=0, tiled=True)  83.5 us
    add x126, other arithmetic, add_pair(): return (earlier_pair[0] + later_pair[0], earlier_pair[1] + later_pair[1])  49.7 us
    all_gather x2, waiting for transfers between devices, prefix(): lax.all_gather(a.astype(kind), axis)  31.2 us
    reduce_sum x1, other arithmetic, attend(): row_sum = jnp.sum(exponent, axis=-1)  21.9 us
  transfers between devices with their start and end apart: 5, of which 3 were waited for; matrix products, arithmetic and copies ran while one was open for 7% of the time, Pallas kernels for 0%

commit v1 on v0

v1 whole, which is shorter than its diff:
```python
import functools

import jax
import jax.numpy as jnp
from jax import lax
from jax.experimental import pallas as pl
from jax.experimental.pallas import tpu as pltpu
from jax.sharding import PartitionSpec as P

D = 128
GROUP = 8
HALF = 64
T = 144
SIDE = 8
BLOCKS = SIDE * SIDE
TOKENS = BLOCKS * T
CHUNK = SIDE * T
ROWS = GROUP * T
PAIR = 2 * T
TILES = ROWS // PAIR
NEG = -1e30
SCALE2 = (D ** -0.5) * 1.4426950408889634
MESH = pl.DeviceIdType.MESH
F32 = jnp.float32
BF16 = jnp.bfloat16


def dot(a, b):
    return lax.dot_general(a, b, (((1,), (0,)), ((), ())), preferred_element_type=F32)


def dot_nt(a, b):
    return lax.dot_general(a, b, (((1,), (1,)), ((), ())), preferred_element_type=F32)


def dot_tn(a, b):
    return lax.dot_general(a, b, (((0,), (0,)), ((), ())), preferred_element_type=F32)


def lanes(rows):
    return lax.broadcasted_iota(jnp.int32, (rows, D), 1)


def halves(x, reduce, neutral):
    plus = lanes(x.shape[0]) < HALF
    a = reduce(jnp.where(plus, x, neutral), axis=1, keepdims=True)
    b = reduce(jnp.where(plus, neutral, x), axis=1, keepdims=True)
    return a, b, plus


def feature_pair(x):
    a, b, plus = halves(x, jnp.max, -jnp.inf)
    e = jnp.exp(x - jnp.where(plus, a, b))
    sa, sb, _ = halves(e, jnp.sum, 0.0)
    return e * jnp.where(plus, 1.0 / sa, 1.0 / sb)


def pair_backward(pn, d):
    a, b, plus = halves(pn * d, jnp.sum, 0.0)
    t = pn * (d - jnp.where(plus, a, b))
    return t - pltpu.roll(t, HALF, 1)


def hi_lo(x):
    hi = x.astype(BF16).astype(F32)
    return hi, x - hi


def place():
    seq = lax.axis_index("seq")
    head = lax.axis_index("head")
    core = head % 2
    y, z = seq % SIDE, seq // SIDE
    f = y + core * (z - y)
    s = z + core * (y - z)
    stride_f = 1 + (SIDE - 1) * core
    stride_s = SIDE - (SIDE - 1) * core
    return seq, head, f, s, stride_f, stride_s


def offset(k):
    return k // 2 - (k % 2) * k


def main_kernel(
    q_ref, k_hbm, v_hbm, wq_ref, wk_ref,
    student_ref, qg_ref, kg_ref, loss_ref,
    kv, qs, qpn, kpn, run_max, acc, prefix, later, low, own_dphi, wk2, loss_acc,
    local_sem, recv_sem, f_sem, s_sem,
):
    seq, head, f, s, stride_f, stride_s = place()

    def rank(ff, ss):
        return (ff * stride_f + ss * stride_s, head)

    f_up, f_dn = rank((f + 1) % SIDE, s), rank((f + SIDE - 1) % SIDE, s)
    s_up, s_dn = rank(f, (s + 1) % SIDE), rank(f, (s + SIDE - 1) % SIDE)

    own = s * SIDE + f
    load_k = pltpu.make_async_copy(k_hbm, kv.at[own, pl.ds(0, T)], local_sem.at[0])
    load_v = pltpu.make_async_copy(v_hbm, kv.at[own, pl.ds(T, T)], local_sem.at[1])
    load_k.start()
    load_v.start()
    barrier = pltpu.get_barrier_semaphore()
    for peer in (f_up, f_dn, s_up, s_dn):
        pl.semaphore_signal(barrier, inc=1, device_id=peer, device_id_type=MESH)
    load_k.wait()
    load_v.wait()
    pl.semaphore_wait(barrier, 4)

    def slot_of(ss, ff):
        return ((ss + 2 * SIDE) % SIDE) * SIDE + (ff + 2 * SIDE) % SIDE

    def copy(slot, sem, peer):
        return pltpu.make_async_remote_copy(
            src_ref=kv.at[slot], dst_ref=kv.at[slot], send_sem=sem, recv_sem=recv_sem.at[slot],
            device_id=peer, device_id_type=MESH,
        )

    def f_copy(slot, way):
        return copy(slot, f_sem.at[way, slot % SIDE], (f_up, f_dn)[way])

    def s_copy(slot, way):
        return copy(slot, s_sem.at[way, slot], (s_up, s_dn)[way])

    def arrived(slot):
        f_copy(slot, 0).wait_recv()

    def spread(slot):
        s_copy(slot, 0).start()
        s_copy(slot, 1).start()

    f_copy(own, 0).start()
    f_copy(own, 1).start()
    spread(own)

    wk = wk_ref[...].astype(F32)
    wk2[...] = jnp.concatenate([wk, -wk], axis=1).astype(BF16)
    k_own = kv[own, pl.ds(0, T), :]
    v_own = kv[own, pl.ds(T, T), :]
    pn_own = feature_pair(dot(k_own, wk2[...]))
    kphi_own = pn_own.astype(BF16)
    ones_t = jnp.ones((T, D), BF16)

    row_token = lax.broadcasted_iota(jnp.int32, (PAIR, T), 0)
    row_token = jnp.where(row_token >= T, row_token - T, row_token)
    causal = lax.broadcasted_iota(jnp.int32, (PAIR, T), 1) <= row_token

    prefix[...] = jnp.zeros_like(prefix)
    later[...] = jnp.zeros_like(later)
    own_dphi[...] = jnp.zeros_like(own_dphi)
    loss_acc[...] = jnp.zeros_like(loss_acc)

    def first(j, carry):
        rows = pl.ds(pl.multiple_of(j * PAIR, PAIR), PAIR)
        q_a = q_ref[:, pl.ds(pl.multiple_of(j * 2 * D, D), D)]
        q_b = q_ref[:, pl.ds(pl.multiple_of(j * 2 * D + D, D), D)]
        q = jnp.concatenate([q_a, q_b], axis=0)
        qs[rows, :] = q
        w = wq_ref[:, pl.ds(pl.multiple_of(j * D, D), D)]
        la, lb = dot(q_a, w), dot(q_b, w)
        plus = lanes(T) < HALF
        xa = jnp.where(plus, la, -pltpu.roll(la, HALF, 1))
        xb = jnp.where(plus, pltpu.roll(lb, HALF, 1), -lb)
        qpn[rows, :] = feature_pair(jnp.concatenate([xa, xb], axis=0))
        scores = jnp.where(causal, dot_nt(q, k_own) * SCALE2, NEG)
        top = jnp.max(scores, axis=1, keepdims=True)
        p = jnp.exp2(scores - top).astype(BF16)
        run_max[rows, :] = jnp.broadcast_to(top, (PAIR, D))
        acc[rows, :] = dot(p, jnp.concatenate([v_own, ones_t], axis=1))

        up = slot_of(s, f - j - 1)
        arrived(up)

        @pl.when(j < 3)
        def _():
            f_copy(up, 0).start()

        spread(up)

        @pl.when(j < 3)
        def _():
            dn = slot_of(s, f + j + 1)
            arrived(dn)

            @pl.when(j < 2)
            def _():
                f_copy(dn, 1).start()

            spread(dn)

        return carry

    lax.fori_loop(0, TILES, first, 0)

    def visible(ss, shape, dim):
        block = lax.broadcasted_iota(jnp.int32, shape, dim) // T
        return ss * stride_s + block * stride_f < seq

    def any_visible(ss):
        return ss * stride_s < seq

    def chunk_kv(ss):
        base = pl.multiple_of(ss * SIDE, SIDE)
        k = kv[pl.ds(base, SIDE), pl.ds(0, T), :].reshape(CHUNK, D)
        v = kv[pl.ds(base, SIDE), pl.ds(T, T), :].reshape(CHUNK, D)
        return k, v

    def step(t, carry):
        @pl.when(t < 24)
        def _():
            h, k = t // 8 + 1, t % 8
            ff = f + offset(k)
            up, dn = slot_of(s - h, ff), slot_of(s + h, ff)
            arrived(up)

            @pl.when(h * 8 + k < 28)
            def _():
                s_copy(up, 0).start()

            arrived(dn)

            @pl.when((h < 3) | (k >= 4))
            def _():
                s_copy(dn, 1).start()

        @pl.when(t == 32)
        def _():
            def last(k, carry):
                arrived(slot_of(s - 4, f + offset(k)))
                return carry

            lax.fori_loop(0, 8, last, 0)

        u = t - 4
        ci, tile = u // 4, u % 4
        ss = (s + offset(ci) + 2 * SIDE) % SIDE

        @pl.when((u >= 0) & any_visible(ss))
        def _():
            k, v = chunk_kv(ss)
            v1 = jnp.concatenate([v, jnp.ones((CHUNK, D), BF16)], axis=1)

            @pl.when(tile == 0)
            def _():
                pn = feature_pair(dot(k, wk2[...]))
                pn = jnp.where(visible(ss, (CHUNK, D), 0), pn, 0.0)
                kpn[pl.ds(pl.multiple_of(ss * CHUNK, CHUNK), CHUNK), :] = pn
                prefix[...] += dot_tn(pn.astype(BF16), v1)

            rows = pl.ds(pl.multiple_of(tile * PAIR, PAIR), PAIR)
            bias = jnp.where(visible(ss, (1, CHUNK), 1), 0.0, NEG)
            scores = dot_nt(qs[rows, :], k) * SCALE2 + bias
            old = run_max[rows, :]
            new = jnp.maximum(old, jnp.max(scores, axis=1, keepdims=True))
            p = jnp.exp2(scores - new[:, :1]).astype(BF16)
            alpha = jnp.exp2(old - new)
            run_max[rows, :] = new
            acc[rows, :] = acc[rows, :] * jnp.concatenate([alpha, alpha], axis=1) + dot(p, v1)

        return carry

    lax.fori_loop(0, 36, step, 0)

    lane_d = lanes(D)
    norm_hi, norm_lo = hi_lo(prefix[:, D:])
    low[...] = jnp.concatenate(
        [prefix[:, :D], jnp.where(lane_d < HALF, norm_hi, norm_lo)], axis=1
    ).astype(BF16)
    lane = lanes(PAIR)
    lane_t = lanes(T)
    pick_t = jnp.where((lane_t == 0) | (lane_t == HALF), 1.0, 0.0).astype(BF16)
    v_pick = jnp.concatenate([v_own, pick_t], axis=1)

    def finish(j, carry):
        rows = pl.ds(pl.multiple_of(j * PAIR, PAIR), PAIR)
        pn = qpn[rows, :]
        phi = pn.astype(BF16)
        intra = jnp.where(causal, dot_nt(phi, kphi_own), 0.0)
        far = dot(phi, low[...])
        numer = dot(intra.astype(BF16), v_own) + far[:, :D]
        far_d = far[:, D:]
        denom = jnp.sum(intra, axis=1, keepdims=True) + (far_d + pltpu.roll(far_d, HALF, 1))
        inv = 1.0 / denom
        student = numer * inv
        student_low = student.astype(BF16)
        student_ref[:, pl.ds(pl.multiple_of(j * 2 * D, D), D)] = student_low[:T]
        student_ref[:, pl.ds(pl.multiple_of(j * 2 * D + D, D), D)] = student_low[T:]
        a = acc[rows, :]
        teacher = (a[:, :D] / a[:, D:]).astype(BF16).astype(F32)
        differ = student - teacher
        loss_acc[...] += jnp.sum((differ * differ).reshape(PAIR // 8, 8, D), axis=0)
        grad = differ * (2.0 / TOKENS)
        numer_low = (grad * inv).astype(BF16)
        dg = -jnp.sum(grad * student, axis=1, keepdims=True) * inv
        dg_hi, dg_lo = hi_lo(dg)
        zero = jnp.zeros_like(dg)
        g_key = jnp.where(lane == 0, dg_hi, jnp.where(lane == HALF, dg_lo, zero)).astype(BF16)
        g_later = jnp.where(lane < HALF, dg_hi, dg_lo).astype(BF16)
        g_norm = jnp.where(
            (lane == 0) | (lane == HALF), dg_hi, jnp.where(lane == 1, dg_lo, zero)
        ).astype(BF16)
        coupling = dot_nt(jnp.concatenate([numer_low, g_key], axis=1), v_pick)
        coupling = jnp.where(causal, coupling, 0.0).astype(BF16)
        later[...] += dot_tn(phi, jnp.concatenate([numer_low, g_later], axis=1))
        own_dphi[...] += dot_tn(coupling, phi)
        dphi = dot(coupling, kphi_own)
        dphi = dphi + dot_nt(jnp.concatenate([numer_low, g_norm], axis=1), low[...])
        dl = pair_backward(pn, dphi).astype(BF16)
        q = qs[rows, :]
        ga, gb = dot_tn(q[:T], dl[:T]), dot_tn(q[T:], dl[T:])
        qg_ref[:, pl.ds(pl.multiple_of(j * D, D), D)] = jnp.where(lane_d < HALF, ga, -gb)
        return carry

    lax.fori_loop(0, TILES, finish, 0)

    norm = later[:, D:]
    norm_hi, norm_lo = hi_lo(norm + pltpu.roll(norm, HALF, 1))
    low[...] = jnp.concatenate(
        [later[:, :D], jnp.where(lane_d < HALF, norm_hi, norm_lo)], axis=1
    ).astype(BF16)
    dl_own = pair_backward(pn_own, own_dphi[...]).astype(BF16)
    kg_ref[...] = dot_tn(k_own, dl_own)
    lane_c = lanes(CHUNK)
    pick_c = jnp.where((lane_c == 0) | (lane_c == HALF), 1.0, 0.0).astype(BF16)

    def back(ss, carry):
        @pl.when(any_visible(ss))
        def _():
            k, v = chunk_kv(ss)
            d = dot_nt(jnp.concatenate([v, pick_c], axis=1), low[...])
            pn = kpn[pl.ds(pl.multiple_of(ss * CHUNK, CHUNK), CHUNK), :]
            kg_ref[...] += dot_tn(k, pair_backward(pn, d).astype(BF16))

        return carry

    lax.fori_loop(0, SIDE, back, 0)
    loss_ref[...] = loss_acc[...]

    def drain_f(j, carry):
        @pl.when(j < 4)
        def _():
            f_copy(slot_of(s, f - j), 0).wait_send()

        @pl.when(j < 3)
        def _():
            f_copy(slot_of(s, f + j), 1).wait_send()

        return carry

    lax.fori_loop(0, 4, drain_f, 0)

    def drain_s(t, carry):
        h, k = t // 8, t % 8
        ff = f + offset(k)

        @pl.when(t < 28)
        def _():
            s_copy(slot_of(s - h, ff), 0).wait_send()

        @pl.when((h < 3) | (k >= 4))
        def _():
            s_copy(slot_of(s + h, ff), 1).wait_send()

        return carry

    lax.fori_loop(0, 32, drain_s, 0)


ORDER = (4, 3, 5, 2, 6, 1, 7)
WIDE = 640


def reduce_kernel(
    qg_ref, kg_ref, loss_ref, qo_ref, ko_ref, lo_ref,
    parts, got1, mid, got2, full, got3, mine, got_loss,
    send1, recv1, send2, recv2, send3, recv3, send4, recv4,
):
    seq, head, f, s, stride_f, stride_s = place()

    def f_rank(j):
        return (((f + j) % SIDE) * stride_f + s * stride_s, head)

    def s_rank(j):
        return (f * stride_f + ((s + j) % SIDE) * stride_s, head)

    def h_rank(j):
        return (seq, (head + j) % SIDE)

    barrier = pltpu.get_barrier_semaphore()
    for rank in (f_rank, s_rank, h_rank):
        for j in range(1, SIDE):
            pl.semaphore_signal(barrier, inc=1, device_id=rank(j), device_id_type=MESH)

    loss = jnp.sum(loss_ref[...], keepdims=True).reshape(1, 1)
    loss_hi, loss_lo = hi_lo(loss)
    lane = lanes(16)
    row = lax.broadcasted_iota(jnp.int32, (16, D), 0)
    extra = jnp.where(row == 0, loss_hi, jnp.where(row == 1, loss_lo, 0.0))
    for i in range(SIDE):
        parts[i, :, pl.ds(0, 512)] = qg_ref[pl.ds(16 * i, 16), :].astype(BF16)
        k = kg_ref[pl.ds(16 * i, 16), :]
        parts[i, :, pl.ds(512, D)] = jnp.where(lane < HALF, k, extra).astype(BF16)
    pl.semaphore_wait(barrier, 3 * (SIDE - 1))

    def copies(src, dst, me, send, recv, rank):
        def make(j):
            return pltpu.make_async_remote_copy(
                src_ref=src(j), dst_ref=dst.at[me], send_sem=send.at[j], recv_sem=recv.at[me],
                device_id=rank(j), device_id_type=MESH,
            )

        def arrival(j):
            slot = (me + j) % SIDE
            return pltpu.make_async_remote_copy(
                src_ref=src(j), dst_ref=dst.at[slot], send_sem=send.at[j], recv_sem=recv.at[slot],
                device_id=rank(j), device_id_type=MESH,
            )

        return make, arrival

    make1, arrive1 = copies(lambda j: parts.at[(f + j) % SIDE], got1, f, send1, recv1, f_rank)
    for j in ORDER:
        make1(j).start()
    total = parts[f].astype(F32)
    for j in range(1, SIDE):
        arrive1(j).wait_recv()
        total = total + got1[(f + j) % SIDE].astype(F32)

    def split(total):
        tail = total[:, 512:]
        value = tail[0:1, HALF:HALF + 1] + tail[1:2, HALF:HALF + 1]
        return tail, value

    def pack(total):
        tail, value = split(total)
        hi, lo = hi_lo(value)
        tail = jnp.where(lane < HALF, tail, jnp.where(row == 0, hi, jnp.where(row == 1, lo, 0.0)))
        return jnp.concatenate([total[:, :512], tail], axis=1).astype(BF16)

    mid[...] = pack(total)
    make2, arrive2 = copies(lambda j: mid, got2, s, send2, recv2, s_rank)
    for j in ORDER:
        make2(j).start()
    total = mid[...].astype(F32)
    for j in range(1, SIDE):
        arrive2(j).wait_recv()
        total = total + got2[(s + j) % SIDE].astype(F32)

    full[...] = total.astype(BF16)
    make3, arrive3 = copies(lambda j: full, got3, f, send3, recv3, f_rank)
    for j in ORDER:
        make3(j).start()
    _, value = split(total)
    mine[...] = jnp.broadcast_to(value, (8, D))
    make4, arrive4 = copies(lambda j: mine, got_loss, head, send4, recv4, h_rank)
    for j in range(1, SIDE):
        make4(j).start()

    def put(i, block):
        rows = pl.ds(pl.multiple_of(i * 16, 16), 16)
        qo_ref[rows, :] = block[:, :512]
        ko_ref[rows, :] = block[:, 512:512 + HALF]

    put(f, total)
    for j in range(1, SIDE):
        arrive3(j).wait_recv()
        slot = (f + j) % SIDE
        put(slot, got3[slot].astype(F32))
    value = mine[...]
    for j in range(1, SIDE):
        arrive4(j).wait_recv()
        value = value + got_loss[(head + j) % SIDE]
    lo_ref[...] = value * (1.0 / TOKENS)
    for make in (make1, make2, make3, make4):
        for j in range(1, SIDE):
            make(j).wait_send()


def local(queries, key_matrix, value_matrix, query_feature_weight, key_feature_weight):
    vmem = pl.BlockSpec(memory_space=pltpu.VMEM)
    anywhere = pl.BlockSpec(memory_space=pl.ANY)
    dma = pltpu.SemaphoreType.DMA
    student, qg, kg, loss = pl.pallas_call(
        main_kernel,
        out_shape=(
            jax.ShapeDtypeStruct((T, GROUP * D), BF16),
            jax.ShapeDtypeStruct((D, GROUP * HALF), F32),
            jax.ShapeDtypeStruct((D, D), F32),
            jax.ShapeDtypeStruct((8, D), F32),
        ),
        in_specs=[vmem, anywhere, anywhere, vmem, vmem],
        out_specs=(vmem, vmem, vmem, vmem),
        scratch_shapes=[
            pltpu.VMEM((BLOCKS, 2 * T, D), BF16),
            pltpu.VMEM((ROWS, D), BF16),
            pltpu.VMEM((ROWS, D), F32),
            pltpu.VMEM((TOKENS, D), F32),
            pltpu.VMEM((ROWS, D), F32),
            pltpu.VMEM((ROWS, 2 * D), F32),
            pltpu.VMEM((D, 2 * D), F32),
            pltpu.VMEM((D, 2 * D), F32),
            pltpu.VMEM((D, 2 * D), BF16),
            pltpu.VMEM((T, D), F32),
            pltpu.VMEM((D, D), BF16),
            pltpu.VMEM((8, D), F32),
            dma((2,)),
            dma((BLOCKS,)),
            dma((2, SIDE)),
            dma((2, BLOCKS)),
        ],
        compiler_params=pltpu.CompilerParams(
            collective_id=0, has_side_effects=True, vmem_limit_bytes=56 * 1024 * 1024
        ),
        name="attend",
    )(queries, key_matrix, value_matrix, query_feature_weight, key_feature_weight)
    qo, ko, lo = pl.pallas_call(
        reduce_kernel,
        out_shape=(
            jax.ShapeDtypeStruct((D, GROUP * HALF), F32),
            jax.ShapeDtypeStruct((D, HALF), F32),
            jax.ShapeDtypeStruct((8, D), F32),
        ),
        in_specs=[vmem] * 3,
        out_specs=(vmem,) * 3,
        scratch_shapes=[
            pltpu.VMEM((SIDE, 16, WIDE), BF16),
            pltpu.VMEM((SIDE, 16, WIDE), BF16),
            pltpu.VMEM((16, WIDE), BF16),
            pltpu.VMEM((SIDE, 16, WIDE), BF16),
            pltpu.VMEM((16, WIDE), BF16),
            pltpu.VMEM((SIDE, 16, WIDE), BF16),
            pltpu.VMEM((8, D), F32),
            pltpu.VMEM((SIDE, 8, D), F32),
        ]
        + [dma((SIDE,))] * 8,
        compiler_params=pltpu.CompilerParams(collective_id=1, has_side_effects=True),
        name="combine",
    )(qg, kg, loss)
    return student, qo, ko, lo[0, 0]


def solution(mesh):
    placed = (
        P("seq", "head"),
        P("seq", "head"),
        P("seq", "head"),
        P(None, "head"),
        P(None, "head"),
    )
    return jax.shard_map(
        local,
        mesh=mesh,
        in_specs=placed,
        out_specs=(P("seq", "head"), P(None, "head"), P(None, "head"), P()),
        check_vma=False,
    )
```

time: 818 us -> 133 us (0.16)
  the two profiles are of different devices: /device:TPU:2 before, /device:TPU:1 now
where the time goes in v1:
time: 133 us; the launch traced here: 132 us
  Pallas kernels  126 us (95%)
  local copies, waits for them, and re-layouts  5.92 us (4%)
    pallas_call x1, Pallas kernels, local(): pl.pallas_call(reduce_kernel, out_shape=(jax.ShapeDtypeStruct((D, GROUP *...  67.1 us
    pallas_call x1, Pallas kernels, local(): pl.pallas_call(main_kernel, out_shape=(jax.ShapeDtypeStruct((T, GROUP * D...  58.6 us
    unnamed x8, local copies, waits for them, and re-layouts  4.73 us

profile of v1, /device:TPU:1, one launch (start us, length us, event | category | flops | bytes accessed | tf_op | source)
XLA Modules:
  0.0 132.3 jit_solution(7704291658539826036)
XLA Ops:
  0.6 1.4 %copy.9.wk_ref = bf16[128,64]{1,0:T(8,128)(2,1)} copy(bf16[128,64]{0,1:T(8,128)(2,1)} %param.9) | data formatting | bytes 32768 | tf_op args[4]
  2.1 58.6 %attend.1 = (bf16[144,1024]{1,0:T(8,128)(2,1)}, f32[128,512]{1,0:T(8,128)}, f32[128,128]{1,0:T(8,128)}, f32[8,128]{1,0:T(8,128)}) custom-call(bf16[144,1024]{1,0:T(8,128)(2,1)} %q_ref.1, bf16[144,128]{1,0:T(8,128)(2,1)} %k_hbm.1, bf16[144,128]{1,0:T(8,128)(2,1)} %v_hbm.1, bf16[128,512]{1,0:T(8,128)(2,1)} %wq_ref.1, bf16[128,64]{1,0:T(8,128)(2,1)} %copy.9.wk_ref), custom_call_target="tpu_custom_call" | custom-call | tf_op jit(solution)/shard_map/attend/pallas_call | solution.py:484
  60.7 0.0 copy-start
  60.7 67.1 %combine.1 = (f32[128,512]{1,0:T(8,128)}, f32[128,64]{1,0:T(8,128)}, f32[8,128]{1,0:T(8,128)}) custom-call(f32[128,512]{1,0:T(8,128)} %get-tuple-element.12.qg_ref, f32[128,128]{1,0:T(8,128)} %get-tuple-element.13.kg_ref, f32[8,128]{1,0:T(8,128)} %get-tuple-element.14.loss_ref), custom_call_target="tpu_custom_call" | custom-call | tf_op jit(solution)/shard_map/combine/pallas_call | solution.py:517
  127.8 1.2 slice.3
  129.0 1.5 %copy.10 = f32[128,64]{0,1:T(8,128)} copy(f32[128,64]{1,0:T(8,128)} %get-tuple-element.20) | data formatting | bytes 65536
  130.5 0.0 copy-done
  130.5 0.0 copy-start.1
  130.5 0.7 copy.13
  131.2 0.3 copy-done.1
  131.6 0.7 copy.14
Async XLA Ops:
  60.7 69.9 %copy-start = (bf16[144,1024]{1,0:T(8,128)(2,1)S(1)}, bf16[144,1024]{1,0:T(8,128)(2,1)}, u32[]{:S(2)}) copy-start(bf16[144,1024]{1,0:T(8,128)(2,1)} %get-tuple-element.26) | copy-start | bytes 884740
  130.5 1.1 copy-start.1

commit v2 on v1

--- a/solution.py
+++ b/solution.py
@@ -61,6 +61,22 @@
     return t - pltpu.roll(t, HALF, 1)
 
 
+def feature_pair_t(x):
+    a = jnp.max(x, axis=0, keepdims=True)
+    b = jnp.min(x, axis=0, keepdims=True)
+    e, g = jnp.exp(x - a), jnp.exp(b - x)
+    e = e * (1.0 / jnp.sum(e, axis=0, keepdims=True))
+    g = g * (1.0 / jnp.sum(g, axis=0, keepdims=True))
+    return e, g
+
+
+def pair_backward_t(e, g, d):
+    dp, dn = d[:HALF], d[HALF:]
+    a = jnp.sum(e * dp, axis=0, keepdims=True)
+    b = jnp.sum(g * dn, axis=0, keepdims=True)
+    return e * (dp - a) - g * (dn - b)
+
+
 def hi_lo(x):
     hi = x.astype(BF16).astype(F32)
     return hi, x - hi
@@ -85,7 +101,7 @@
 def main_kernel(
     q_ref, k_hbm, v_hbm, wq_ref, wk_ref,
     student_ref, qg_ref, kg_ref, loss_ref,
-    kv, qs, qpn, kpn, run_max, acc, prefix, later, low, own_dphi, wk2, loss_acc,
+    kv, qs, qpn, kpn, run_max, acc, scores, probs, prefix, later, low, own_dphi, wkt, loss_acc,
     local_sem, recv_sem, f_sem, s_sem,
 ):
     seq, head, f, s, stride_f, stride_s = place()
@@ -134,12 +150,11 @@
     f_copy(own, 1).start()
     spread(own)
 
-    wk = wk_ref[...].astype(F32)
-    wk2[...] = jnp.concatenate([wk, -wk], axis=1).astype(BF16)
+    wkt[...] = wk_ref[...].astype(F32).T.astype(BF16)
     k_own = kv[own, pl.ds(0, T), :]
     v_own = kv[own, pl.ds(T, T), :]
-    pn_own = feature_pair(dot(k_own, wk2[...]))
-    kphi_own = pn_own.astype(BF16)
+    e_own, g_own = feature_pair_t(dot_nt(wkt[...], k_own))
+    kphi_own = jnp.concatenate([e_own, g_own], axis=0).astype(BF16)
     ones_t = jnp.ones((T, D), BF16)
 
     row_token = lax.broadcasted_iota(jnp.int32, (PAIR, T), 0)
@@ -193,8 +208,8 @@
 
     lax.fori_loop(0, TILES, first, 0)
 
-    def visible(ss, shape, dim):
-        block = lax.broadcasted_iota(jnp.int32, shape, dim) // T
+    def visible(ss):
+        block = lax.broadcasted_iota(jnp.int32, (1, CHUNK), 1) // T
         return ss * stride_s + block * stride_f < seq
 
     def any_visible(ss):
@@ -206,61 +221,82 @@
         v = kv[pl.ds(base, SIDE), pl.ds(T, T), :].reshape(CHUNK, D)
         return k, v
 
-    def step(t, carry):
-        @pl.when(t < 24)
-        def _():
-            h, k = t // 8 + 1, t % 8
-            ff = f + offset(k)
-            up, dn = slot_of(s - h, ff), slot_of(s + h, ff)
-            arrived(up)
-
-            @pl.when(h * 8 + k < 28)
-            def _():
-                s_copy(up, 0).start()
-
-            arrived(dn)
-
-            @pl.when((h < 3) | (k >= 4))
-            def _():
-                s_copy(dn, 1).start()
-
-        @pl.when(t == 32)
-        def _():
-            def last(k, carry):
-                arrived(slot_of(s - 4, f + offset(k)))
-                return carry
-
+    def relay(n, carry):
+        h, k = n // 8 + 1, n % 8
+        ff = f + offset(k)
+        up, dn = slot_of(s - h, ff), slot_of(s + h, ff)
+        arrived(up)
+
+        @pl.when(n < 20)
+        def _():
+            s_copy(up, 0).start()
+
+        arrived(dn)
+
+        @pl.when((h < 3) | (k >= 4))
+        def _():
+            s_copy(dn, 1).start()
+
+        return carry
+
+    def last(k, carry):
+        arrived(slot_of(s - 4, f + offset(k)))
+        return carry
+
+    def step(ci, carry):
+        @pl.when(ci < 6)
+        def _():
+            lax.fori_loop(4 * ci, 4 * ci + 4, relay, 0)
+
+        @pl.when(ci == 7)
+        def _():
             lax.fori_loop(0, 8, last, 0)
 
-        u = t - 4
-        ci, tile = u // 4, u % 4
         ss = (s + offset(ci) + 2 * SIDE) % SIDE
 
-        @pl.when((u >= 0) & any_visible(ss))
+        @pl.when(any_visible(ss))
         def _():
             k, v = chunk_kv(ss)
             v1 = jnp.concatenate([v, jnp.ones((CHUNK, D), BF16)], axis=1)
-
-            @pl.when(tile == 0)
-            def _():
-                pn = feature_pair(dot(k, wk2[...]))
-                pn = jnp.where(visible(ss, (CHUNK, D), 0), pn, 0.0)
-                kpn[pl.ds(pl.multiple_of(ss * CHUNK, CHUNK), CHUNK), :] = pn
-                prefix[...] += dot_tn(pn.astype(BF16), v1)
-
-            rows = pl.ds(pl.multiple_of(tile * PAIR, PAIR), PAIR)
-            bias = jnp.where(visible(ss, (1, CHUNK), 1), 0.0, NEG)
-            scores = dot_nt(qs[rows, :], k) * SCALE2 + bias
-            old = run_max[rows, :]
-            new = jnp.maximum(old, jnp.max(scores, axis=1, keepdims=True))
-            p = jnp.exp2(scores - new[:, :1]).astype(BF16)
-            alpha = jnp.exp2(old - new)
-            run_max[rows, :] = new
-            acc[rows, :] = acc[rows, :] * jnp.concatenate([alpha, alpha], axis=1) + dot(p, v1)
-
-        return carry
-
-    lax.fori_loop(0, 36, step, 0)
+            seen = visible(ss)
+            bias = jnp.where(seen, 0.0, NEG)
+            cuts = [(i, min(256, CHUNK - i)) for i in range(0, CHUNK, 256)]
+
+            def score(r):
+                rows = pl.ds(r * PAIR, PAIR)
+                q = qs[rows, :]
+                top = None
+                for i, n in cuts:
+                    x = dot_nt(q, k[i:i + n]) * SCALE2 + bias[:, i:i + n]
+                    scores[r % 2, :, pl.ds(i, n)] = x
+                    for c in range(0, n, D):
+                        top = x[:, c:c + D] if top is None else jnp.maximum(top, x[:, c:c + D])
+                old = run_max[rows, :]
+                new = jnp.maximum(old, jnp.max(top, axis=1, keepdims=True))
+                run_max[rows, :] = new
+                return new, jnp.exp2(old - new)
+
+            def weigh(r, new, alpha):
+                rows = pl.ds(r * PAIR, PAIR)
+                for i in range(0, CHUNK, D):
+                    x = scores[r % 2, :, pl.ds(i, D)]
+                    probs[r % 2, :, pl.ds(i, D)] = jnp.exp2(x - new).astype(BF16)
+                out = dot(probs[r % 2], v1)
+                acc[rows, :] = acc[rows, :] * jnp.concatenate([alpha, alpha], axis=1) + out
+
+            held = score(0)
+            e, g = feature_pair_t(dot_nt(wkt[...], k))
+            pn = jnp.where(seen, jnp.concatenate([e, g], axis=0), 0.0)
+            kpn[ss] = pn
+            prefix[...] += dot(pn.astype(BF16), v1)
+            for r in range(TILES):
+                ahead = score(r + 1) if r + 1 < TILES else None
+                weigh(r, *held)
+                held = ahead
+
+        return carry
+
+    lax.fori_loop(0, SIDE, step, 0)
 
     lane_d = lanes(D)
     norm_hi, norm_lo = hi_lo(prefix[:, D:])
@@ -276,7 +312,7 @@
         rows = pl.ds(pl.multiple_of(j * PAIR, PAIR), PAIR)
         pn = qpn[rows, :]
         phi = pn.astype(BF16)
-        intra = jnp.where(causal, dot_nt(phi, kphi_own), 0.0)
+        intra = jnp.where(causal, dot(phi, kphi_own), 0.0)
         far = dot(phi, low[...])
         numer = dot(intra.astype(BF16), v_own) + far[:, :D]
         far_d = far[:, D:]
@@ -303,8 +339,8 @@
         coupling = dot_nt(jnp.concatenate([numer_low, g_key], axis=1), v_pick)
         coupling = jnp.where(causal, coupling, 0.0).astype(BF16)
         later[...] += dot_tn(phi, jnp.concatenate([numer_low, g_later], axis=1))
-        own_dphi[...] += dot_tn(coupling, phi)
-        dphi = dot(coupling, kphi_own)
+        own_dphi[...] += dot_tn(phi, coupling)
+        dphi = dot_nt(coupling, kphi_own)
         dphi = dphi + dot_nt(jnp.concatenate([numer_low, g_norm], axis=1), low[...])
         dl = pair_backward(pn, dphi).astype(BF16)
         q = qs[rows, :]
@@ -319,8 +355,7 @@
     low[...] = jnp.concatenate(
         [later[:, :D], jnp.where(lane_d < HALF, norm_hi, norm_lo)], axis=1
     ).astype(BF16)
-    dl_own = pair_backward(pn_own, own_dphi[...]).astype(BF16)
-    kg_ref[...] = dot_tn(k_own, dl_own)
+    kg_ref[...] = dot(pair_backward_t(e_own, g_own, own_dphi[...]).astype(BF16), k_own)
     lane_c = lanes(CHUNK)
     pick_c = jnp.where((lane_c == 0) | (lane_c == HALF), 1.0, 0.0).astype(BF16)
 
@@ -328,9 +363,10 @@
         @pl.when(any_visible(ss))
         def _():
             k, v = chunk_kv(ss)
-            d = dot_nt(jnp.concatenate([v, pick_c], axis=1), low[...])
-            pn = kpn[pl.ds(pl.multiple_of(ss * CHUNK, CHUNK), CHUNK), :]
-            kg_ref[...] += dot_tn(k, pair_backward(pn, d).astype(BF16))
+            d = dot_nt(low[...], jnp.concatenate([v, pick_c], axis=1))
+            kg_ref[...] += dot(
+                pair_backward_t(kpn[ss, :HALF], kpn[ss, HALF:], d).astype(BF16), k
+            )
 
         return carry
 
@@ -394,13 +430,12 @@
 
     loss = jnp.sum(loss_ref[...], keepdims=True).reshape(1, 1)
     loss_hi, loss_lo = hi_lo(loss)
-    lane = lanes(16)
-    row = lax.broadcasted_iota(jnp.int32, (16, D), 0)
+    row = lax.broadcasted_iota(jnp.int32, (8, D), 0)
     extra = jnp.where(row == 0, loss_hi, jnp.where(row == 1, loss_lo, 0.0))
     for i in range(SIDE):
         parts[i, :, pl.ds(0, 512)] = qg_ref[pl.ds(16 * i, 16), :].astype(BF16)
-        k = kg_ref[pl.ds(16 * i, 16), :]
-        parts[i, :, pl.ds(512, D)] = jnp.where(lane < HALF, k, extra).astype(BF16)
+        k = kg_ref[pl.ds(8 * i, 8), :]
+        parts[i, :, pl.ds(512, D)] = jnp.concatenate([k, extra], axis=0).astype(BF16)
     pl.semaphore_wait(barrier, 3 * (SIDE - 1))
 
     def copies(src, dst, me, send, recv, rank):
@@ -427,15 +462,14 @@
         arrive1(j).wait_recv()
         total = total + got1[(f + j) % SIDE].astype(F32)
 
-    def split(total):
-        tail = total[:, 512:]
-        value = tail[0:1, HALF:HALF + 1] + tail[1:2, HALF:HALF + 1]
-        return tail, value
+    def value_of(total):
+        tail = total[8:, 512:]
+        return tail[0:1, 0:1] + tail[1:2, 0:1]
 
     def pack(total):
-        tail, value = split(total)
-        hi, lo = hi_lo(value)
-        tail = jnp.where(lane < HALF, tail, jnp.where(row == 0, hi, jnp.where(row == 1, lo, 0.0)))
+        hi, lo = hi_lo(value_of(total))
+        extra = jnp.where(row == 0, hi, jnp.where(row == 1, lo, 0.0))
+        tail = jnp.concatenate([total[:8, 512:], extra], axis=0)
         return jnp.concatenate([total[:, :512], tail], axis=1).astype(BF16)
 
     mid[...] = pack(total)
@@ -451,16 +485,14 @@
     make3, arrive3 = copies(lambda j: full, got3, f, send3, recv3, f_rank)
     for j in ORDER:
         make3(j).start()
-    _, value = split(total)
-    mine[...] = jnp.broadcast_to(value, (8, D))
+    mine[...] = jnp.broadcast_to(value_of(total), (8, D))
     make4, arrive4 = copies(lambda j: mine, got_loss, head, send4, recv4, h_rank)
     for j in range(1, SIDE):
         make4(j).start()
 
     def put(i, block):
-        rows = pl.ds(pl.multiple_of(i * 16, 16), 16)
-        qo_ref[rows, :] = block[:, :512]
-        ko_ref[rows, :] = block[:, 512:512 + HALF]
+        qo_ref[pl.ds(pl.multiple_of(i * 16, 16), 16), :] = block[:, :512]
+        ko_ref[pl.ds(pl.multiple_of(i * 8, 8), 8), :] = block[:8, 512:]
 
     put(f, total)
     for j in range(1, SIDE):
@@ -477,16 +509,16 @@
             make(j).wait_send()
 
 
-def local(queries, key_matrix, value_matrix, query_feature_weight, key_feature_weight):
+def attend(queries, key_matrix, value_matrix, query_feature_weight, key_feature_weight):
     vmem = pl.BlockSpec(memory_space=pltpu.VMEM)
     anywhere = pl.BlockSpec(memory_space=pl.ANY)
     dma = pltpu.SemaphoreType.DMA
-    student, qg, kg, loss = pl.pallas_call(
+    return pl.pallas_call(
         main_kernel,
         out_shape=(
             jax.ShapeDtypeStruct((T, GROUP * D), BF16),
             jax.ShapeDtypeStruct((D, GROUP * HALF), F32),
-            jax.ShapeDtypeStruct((D, D), F32),
+            jax.ShapeDtypeStruct((HALF, D), F32),
             jax.ShapeDtypeStruct((8, D), F32),
         ),
         in_specs=[vmem, anywhere, anywhere, vmem, vmem],
@@ -495,14 +527,16 @@
             pltpu.VMEM((BLOCKS, 2 * T, D), BF16),
             pltpu.VMEM((ROWS, D), BF16),
             pltpu.VMEM((ROWS, D), F32),
-            pltpu.VMEM((TOKENS, D), F32),
+            pltpu.VMEM((SIDE, D, CHUNK), F32),
             pltpu.VMEM((ROWS, D), F32),
             pltpu.VMEM((ROWS, 2 * D), F32),
+            pltpu.VMEM((2, PAIR, CHUNK), F32),
+            pltpu.VMEM((2, PAIR, CHUNK), BF16),
             pltpu.VMEM((D, 2 * D), F32),
             pltpu.VMEM((D, 2 * D), F32),
             pltpu.VMEM((D, 2 * D), BF16),
-            pltpu.VMEM((T, D), F32),
-            pltpu.VMEM((D, D), BF16),
+            pltpu.VMEM((D, T), F32),
+            pltpu.VMEM((HALF, D), BF16),
             pltpu.VMEM((8, D), F32),
             dma((2,)),
             dma((BLOCKS,)),
@@ -514,11 +548,16 @@
         ),
         name="attend",
     )(queries, key_matrix, value_matrix, query_feature_weight, key_feature_weight)
-    qo, ko, lo = pl.pallas_call(
+
+
+def combine(qg, kg, loss):
+    vmem = pl.BlockSpec(memory_space=pltpu.VMEM)
+    dma = pltpu.SemaphoreType.DMA
+    return pl.pallas_call(
         reduce_kernel,
         out_shape=(
             jax.ShapeDtypeStruct((D, GROUP * HALF), F32),
-            jax.ShapeDtypeStruct((D, HALF), F32),
+            jax.ShapeDtypeStruct((HALF, D), F32),
             jax.ShapeDtypeStruct((8, D), F32),
         ),
         in_specs=[vmem] * 3,
@@ -537,7 +576,12 @@
         compiler_params=pltpu.CompilerParams(collective_id=1, has_side_effects=True),
         name="combine",
     )(qg, kg, loss)
-    return student, qo, ko, lo[0, 0]
+
+
+def local(*operands):
+    student, qg, kg, loss = attend(*operands)
+    qo, ko, lo = combine(qg, kg, loss)
+    return student, qo, ko.T, lo[0, 0]
 
 
 def solution(mesh):

time: 133 us -> 96.3 us (0.72)
  Pallas kernels: 126 us -> 90.1 us
    pallas_call x2, Pallas kernels: 126 us -> 90.1 us  [the longest x1 53.1 us: attend(): pl.pallas_call(main_kernel, out_shape=(jax.ShapeDtypeStruct((T, GROUP * D...]
    unnamed x8 -> x10, local copies, waits for them, and re-layouts: 4.73 us -> 3.87 us
where the time goes in v2:
time: 96.3 us; the launch traced here: 95.8 us
  Pallas kernels  90.1 us (94%)
  local copies, waits for them, and re-layouts  5.05 us (5%)
    pallas_call x1, Pallas kernels, attend(): pl.pallas_call(main_kernel, out_shape=(jax.ShapeDtypeStruct((T, GROUP * D...  53.1 us
    pallas_call x1, Pallas kernels, combine(): pl.pallas_call(reduce_kernel, out_shape=(jax.ShapeDtypeStruct((D, GROUP *...  37 us
    unnamed x10, local copies, waits for them, and re-layouts  3.87 us

profile of v2, /device:TPU:1, one launch (start us, length us, event | category | flops | bytes accessed | tf_op | source)
XLA Modules:
  0.0 95.8 jit_solution(5913135372526776122)
XLA Ops:
  0.6 1.4 %copy.9.wk_ref = bf16[128,64]{1,0:T(8,128)(2,1)} copy(bf16[128,64]{0,1:T(8,128)(2,1)} %param.9) | data formatting | bytes 32768 | tf_op args[4]
  2.1 53.1 %attend.1 = (bf16[144,1024]{1,0:T(8,128)(2,1)}, f32[128,512]{1,0:T(8,128)}, f32[64,128]{1,0:T(8,128)}, f32[8,128]{1,0:T(8,128)}) custom-call(bf16[144,1024]{1,0:T(8,128)(2,1)} %q_ref.1, bf16[144,128]{1,0:T(8,128)(2,1)} %k_hbm.1, bf16[144,128]{1,0:T(8,128)(2,1)} %v_hbm.1, bf16[128,512]{1,0:T(8,128)(2,1)} %wq_ref.1, bf16[128,64]{1,0:T(8,128)(2,1)} %copy.9.wk_ref), custom_call_target="tpu_custom_call" | custom-call | tf_op jit(solution)/shard_map/attend/pallas_call | solution.py:516
  55.2 0.0 copy-start
  55.2 37.0 %combine.1 = (f32[128,512]{1,0:T(8,128)}, f32[64,128]{1,0:T(8,128)}, f32[8,128]{1,0:T(8,128)}) custom-call(f32[128,512]{1,0:T(8,128)} %get-tuple-element.12.qg_ref, f32[64,128]{1,0:T(8,128)} %get-tuple-element.13.kg_ref, f32[8,128]{1,0:T(8,128)} %get-tuple-element.14.loss_ref), custom_call_target="tpu_custom_call" | custom-call | tf_op jit(solution)/shard_map/combine/pallas_call | solution.py:556
  92.2 1.2 %slice.3 = f32[1,1]{1,0:T(1,128)} slice(f32[8,128]{1,0:T(8,128)} %get-tuple-element.17), slice={[0:1], [0:1]} | slice | bytes 8 | tf_op jit(solution)/shard_map/slice | solution.py:584
  93.4 0.0 copy-done
  93.4 0.0 copy-start.1
  93.4 0.7 copy.13
  94.1 0.3 copy-done.1
  94.5 0.0 copy-start.2
  94.5 0.7 copy.14
  95.2 0.1 copy-done.2
  95.2 0.6 copy.15
Async XLA Ops:
  55.2 38.2 %copy-start = (bf16[144,1024]{1,0:T(8,128)(2,1)S(1)}, bf16[144,1024]{1,0:T(8,128)(2,1)}, u32[]{:S(2)}) copy-start(bf16[144,1024]{1,0:T(8,128)(2,1)} %get-tuple-element.22) | copy-start | bytes 884740
  93.4 1.1 %copy-start.1 = (f32[128,512]{1,0:T(8,128)S(1)}, f32[128,512]{1,0:T(8,128)}, u32[]{:S(2)}) copy-start(f32[128,512]{1,0:T(8,128)} %get-tuple-element.23) | copy-start | bytes 786436
  94.5 0.8 copy-start.2

commit v3 on v2

v3 whole, which is shorter than its diff:
```python
import functools

import jax
import jax.numpy as jnp
from jax import lax
from jax.experimental import pallas as pl
from jax.experimental.pallas import tpu as pltpu
from jax.sharding import PartitionSpec as P

D = 128
GROUP = 8
HALF = 64
T = 144
SIDE = 8
BLOCKS = SIDE * SIDE
TOKENS = BLOCKS * T
CHUNK = SIDE * T
ROWS = GROUP * T
PAIR = 2 * T
TILES = ROWS // PAIR
NEG = -1e30
SCALE2 = (D ** -0.5) * 1.4426950408889634
MESH = pl.DeviceIdType.MESH
F32 = jnp.float32
BF16 = jnp.bfloat16


def dot(a, b):
    return lax.dot_general(a, b, (((1,), (0,)), ((), ())), preferred_element_type=F32)


def dot_nt(a, b):
    return lax.dot_general(a, b, (((1,), (1,)), ((), ())), preferred_element_type=F32)


def dot_tn(a, b):
    return lax.dot_general(a, b, (((0,), (0,)), ((), ())), preferred_element_type=F32)


def lanes(rows):
    return lax.broadcasted_iota(jnp.int32, (rows, D), 1)


def halves(x, reduce, neutral):
    plus = lanes(x.shape[0]) < HALF
    a = reduce(jnp.where(plus, x, neutral), axis=1, keepdims=True)
    b = reduce(jnp.where(plus, neutral, x), axis=1, keepdims=True)
    return a, b, plus


def feature_pair(x):
    a, b, plus = halves(x, jnp.max, -jnp.inf)
    e = jnp.exp(x - jnp.where(plus, a, b))
    sa, sb, _ = halves(e, jnp.sum, 0.0)
    return e * jnp.where(plus, 1.0 / sa, 1.0 / sb)


def pair_backward(pn, d):
    a, b, plus = halves(pn * d, jnp.sum, 0.0)
    t = pn * (d - jnp.where(plus, a, b))
    return t - pltpu.roll(t, HALF, 1)


def feature_pair_t(x):
    a = jnp.max(x, axis=0, keepdims=True)
    b = jnp.min(x, axis=0, keepdims=True)
    e, g = jnp.exp(x - a), jnp.exp(b - x)
    e = e * (1.0 / jnp.sum(e, axis=0, keepdims=True))
    g = g * (1.0 / jnp.sum(g, axis=0, keepdims=True))
    return e, g


def pair_backward_t(e, g, d):
    dp, dn = d[:HALF], d[HALF:]
    a = jnp.sum(e * dp, axis=0, keepdims=True)
    b = jnp.sum(g * dn, axis=0, keepdims=True)
    return e * (dp - a) - g * (dn - b)


def hi_lo(x):
    hi = x.astype(BF16).astype(F32)
    return hi, x - hi


def place():
    seq = lax.axis_index("seq")
    head = lax.axis_index("head")
    core = head % 2
    y, z = seq % SIDE, seq // SIDE
    f = y + core * (z - y)
    s = z + core * (y - z)
    stride_f = 1 + (SIDE - 1) * core
    stride_s = SIDE - (SIDE - 1) * core
    return seq, head, f, s, stride_f, stride_s


def offset(k):
    return k // 2 - (k % 2) * k


FAR = (4, 3, 5, 2, 6, 1, 7)
NEAR = FAR[::-1]


def plan():
    waves = [[("own", 0, 0, 0)]]
    for w in range(1, 9):
        wave = []
        if w <= 4:
            wave.append(("f", 0, 0, 2 * w - 1))
        if w <= 3:
            wave.append(("f", 1, 0, 2 * w))
        for h in range(1, 5):
            d = w - h
            if not 0 <= d <= 4:
                continue
            for k in (2 * d - 1, 2 * d) if 1 <= d <= 3 else ((0,) if d == 0 else (7,)):
                if h <= 3 or k < 4:
                    wave.append(("s", 0, h, k))
                if h <= 3 or k >= 4:
                    wave.append(("s", 1, h, k))
        waves.append(wave)
    return waves


WAVES = plan()
SLOT = {}
SHIFT = []
for item in (item for wave in WAVES for item in wave):
    ring, way, hops, k = item
    SLOT[(0, 0, k) if hops == 0 else (way, hops, k)] = len(SHIFT)
    SHIFT.append((-hops if way == 0 else hops, offset(k)))
FLAT = [item for wave in WAVES for item in wave]
BEFORE = [FLAT[a:b] for a, b in ((5, 13), (13, 25), (25, 32), (32, 39), (39, 45), (45, 51), (51, 59), (59, 64))]


def sends_after(item):
    ring, way, hops, k = item
    out = []
    if hops == 0:
        mine = SLOT[(0, 0, k)]
        far = abs(offset(k))
        for step in (0, 1):
            if (ring == "own" or step == way) and far < (4 if step == 0 else 3):
                there = SLOT[(0, 0, 2 * (far + 1) - 1 if step == 0 else 2 * (far + 1))]
                out.append((mine, there, 0, step))
        for step in (0, 1):
            out.append((mine, SLOT[(step, 1, k)], 1, step))
    else:
        there = (way, hops + 1, k)
        if there in SLOT:
            out.append((SLOT[(way, hops, k)], SLOT[there], 1, way))
    return out


SENDS = [send for item in FLAT for send in sends_after(item)]


def main_kernel(
    q_ref, k_hbm, v_hbm, wq_ref, wk_ref,
    student_ref, qg_ref, kg_ref, loss_ref,
    kv, qs, qpn, kpn, run_max, acc, scores, probs, bias_all, prefix, later, low, own_dphi, loss_acc, kg_acc,
    parts, got1, mid, got2, full, got3, kparts, kgot1, kmid, kgot2, kfull, kgot3, mine, got_loss,
    local_sem, recv_sem, send_sem, out_sem, in_sem,
):
    seq, head, f, s, stride_f, stride_s = place()

    def rank(ff, ss):
        return (ff * stride_f + ss * stride_s, head)

    f_up, f_dn = rank((f + 1) % SIDE, s), rank((f + SIDE - 1) % SIDE, s)
    s_up, s_dn = rank(f, (s + 1) % SIDE), rank(f, (s + SIDE - 1) % SIDE)

    load_k = pltpu.make_async_copy(k_hbm, kv.at[0, pl.ds(0, T)], local_sem.at[0])
    load_v = pltpu.make_async_copy(v_hbm, kv.at[0, pl.ds(T, T)], local_sem.at[1])
    load_k.start()
    load_v.start()
    def f_rank(j):
        return rank((f + j) % SIDE, s)

    def s_rank(j):
        return rank(f, (s + j) % SIDE)

    def h_rank(j):
        return (seq, (head + j) % SIDE)

    barrier = pltpu.get_barrier_semaphore()
    for to in (f_rank, s_rank, h_rank):
        for j in range(1, SIDE):
            pl.semaphore_signal(barrier, inc=1, device_id=to(j), device_id_type=MESH)
    load_k.wait()
    load_v.wait()
    pl.semaphore_wait(barrier, 3 * (SIDE - 1))

    peers = ((f_up, f_dn), (s_up, s_dn))

    def copy(send):
        source, target, ring, way = send
        return pltpu.make_async_remote_copy(
            src_ref=kv.at[source], dst_ref=kv.at[target],
            send_sem=send_sem.at[SENDS.index(send)], recv_sem=recv_sem.at[target],
            device_id=peers[ring][way], device_id_type=MESH,
        )

    def forward(item):
        for send in sends_after(item):
            copy(send).start()

    def relay(items):
        for item in items:
            _, way, hops, k = item
            slot = SLOT[(0, 0, k) if hops == 0 else (way, hops, k)]
            pltpu.make_async_remote_copy(
                src_ref=kv.at[slot], dst_ref=kv.at[slot], send_sem=send_sem.at[0],
                recv_sem=recv_sem.at[slot], device_id=s_up, device_id_type=MESH,
            ).wait_recv()
            forward(item)

    forward(FLAT[0])

    block = lax.broadcasted_iota(jnp.int32, (1, CHUNK), 1) // T
    on = []
    for n in range(SIDE):
        row = jnp.zeros((1, CHUNK), F32)
        count = 0
        for j in range(SIDE):
            ds, df = SHIFT[n * SIDE + j]
            there = ((s + ds + SIDE) % SIDE) * stride_s + ((f + df + SIDE) % SIDE) * stride_f
            hidden = there >= seq
            row = jnp.where((block == j) & hidden, NEG, row)
            count = count + jnp.where(hidden, 0, 1)
        bias_all[n] = row
        on.append(count)

    def active(ci):
        return sum(jnp.where(ci == n, on[n], 0) for n in range(SIDE)) > 0

    k_own = kv[0, pl.ds(0, T), :]
    v_own = kv[0, pl.ds(T, T), :]
    e_own, g_own = feature_pair_t(dot_nt(wk_ref[...], k_own))
    kphi_own = jnp.concatenate([e_own, g_own], axis=0).astype(BF16)
    ones_t = jnp.ones((T, D), BF16)

    row_token = lax.broadcasted_iota(jnp.int32, (PAIR, T), 0)
    row_token = jnp.where(row_token >= T, row_token - T, row_token)
    causal = lax.broadcasted_iota(jnp.int32, (PAIR, T), 1) <= row_token

    prefix[...] = jnp.zeros_like(prefix)
    later[...] = jnp.zeros_like(later)
    own_dphi[...] = jnp.zeros_like(own_dphi)
    loss_acc[...] = jnp.zeros_like(loss_acc)

    def first(j, carry):
        @pl.when(j == 3)
        def _():
            relay(FLAT[1:5])

        rows = pl.ds(pl.multiple_of(j * PAIR, PAIR), PAIR)
        q_a = q_ref[:, pl.ds(pl.multiple_of(j * 2 * D, D), D)]
        q_b = q_ref[:, pl.ds(pl.multiple_of(j * 2 * D + D, D), D)]
        q = jnp.concatenate([q_a, q_b], axis=0)
        qs[rows, :] = q
        w = wq_ref[:, pl.ds(pl.multiple_of(j * D, D), D)]
        la, lb = dot(q_a, w), dot(q_b, w)
        plus = lanes(T) < HALF
        xa = jnp.where(plus, la, -pltpu.roll(la, HALF, 1))
        xb = jnp.where(plus, pltpu.roll(lb, HALF, 1), -lb)
        qpn[rows, :] = feature_pair(jnp.concatenate([xa, xb], axis=0))
        scores = jnp.where(causal, dot_nt(q, k_own) * SCALE2, NEG)
        top = jnp.max(scores, axis=1, keepdims=True)
        p = jnp.exp2(scores - top).astype(BF16)
        run_max[rows, :] = jnp.broadcast_to(top, (PAIR, D))
        acc[rows, :] = dot(p, jnp.concatenate([v_own, ones_t], axis=1))

        return carry

    lax.fori_loop(0, TILES, first, 0)

    def chunk_kv(ss):
        base = pl.multiple_of(ss * SIDE, SIDE)
        k = kv[pl.ds(base, SIDE), pl.ds(0, T), :].reshape(CHUNK, D)
        v = kv[pl.ds(base, SIDE), pl.ds(T, T), :].reshape(CHUNK, D)
        return k, v

    def step(ci, carry):
        for n in range(SIDE):
            pl.when(ci == n)(functools.partial(relay, BEFORE[n]))

        @pl.when(active(ci))
        def _():
            k, v = chunk_kv(ci)
            v1 = jnp.concatenate([v, jnp.ones((CHUNK, D), BF16)], axis=1)
            bias = bias_all[ci]
            seen = bias == 0.0
            cuts = [(i, min(256, CHUNK - i)) for i in range(0, CHUNK, 256)]

            def score(r):
                rows = pl.ds(r * PAIR, PAIR)
                q = qs[rows, :]
                top = None
                for i, n in cuts:
                    x = dot_nt(q, k[i:i + n]) * SCALE2 + bias[:, i:i + n]
                    scores[r % 2, :, pl.ds(i, n)] = x
                    for c in range(0, n, D):
                        top = x[:, c:c + D] if top is None else jnp.maximum(top, x[:, c:c + D])
                old = run_max[rows, :]
                new = jnp.maximum(old, jnp.max(top, axis=1, keepdims=True))
                run_max[rows, :] = new
                return new, jnp.exp2(old - new)

            def weigh(r, new, alpha):
                rows = pl.ds(r * PAIR, PAIR)
                for i in range(0, CHUNK, D):
                    x = scores[r % 2, :, pl.ds(i, D)]
                    probs[r % 2, :, pl.ds(i, D)] = jnp.exp2(x - new).astype(BF16)
                out = dot(probs[r % 2], v1)
                acc[rows, :] = acc[rows, :] * jnp.concatenate([alpha, alpha], axis=1) + out

            held = score(0)
            e, g = feature_pair_t(dot_nt(wk_ref[...], k))
            pn = jnp.where(seen, jnp.concatenate([e, g], axis=0), 0.0)
            kpn[ci] = pn
            prefix[...] += dot(pn.astype(BF16), v1)
            for r in range(TILES):
                ahead = score(r + 1) if r + 1 < TILES else None
                weigh(r, *held)
                held = ahead

        return carry

    lax.fori_loop(0, SIDE, step, 0)

    lane_d = lanes(D)
    norm_hi, norm_lo = hi_lo(prefix[:, D:])
    low[...] = jnp.concatenate(
        [prefix[:, :D], jnp.where(lane_d < HALF, norm_hi, norm_lo)], axis=1
    ).astype(BF16)
    lane = lanes(PAIR)
    lane_t = lanes(T)
    pick_t = jnp.where((lane_t == 0) | (lane_t == HALF), 1.0, 0.0).astype(BF16)
    v_pick = jnp.concatenate([v_own, pick_t], axis=1)

    def finish(j, carry):
        rows = pl.ds(pl.multiple_of(j * PAIR, PAIR), PAIR)
        pn = qpn[rows, :]
        phi = pn.astype(BF16)
        intra = jnp.where(causal, dot(phi, kphi_own), 0.0)
        far = dot(phi, low[...])
        numer = dot(intra.astype(BF16), v_own) + far[:, :D]
        far_d = far[:, D:]
        denom = jnp.sum(intra, axis=1, keepdims=True) + (far_d + pltpu.roll(far_d, HALF, 1))
        inv = 1.0 / denom
        student = numer * inv
        student_low = student.astype(BF16)
        student_ref[:, pl.ds(pl.multiple_of(j * 2 * D, D), D)] = student_low[:T]
        student_ref[:, pl.ds(pl.multiple_of(j * 2 * D + D, D), D)] = student_low[T:]
        a = acc[rows, :]
        teacher = (a[:, :D] / a[:, D:]).astype(BF16).astype(F32)
        differ = student - teacher
        loss_acc[...] += jnp.sum((differ * differ).reshape(PAIR // 8, 8, D), axis=0)
        grad = differ * (2.0 / TOKENS)
        numer_low = (grad * inv).astype(BF16)
        dg = -jnp.sum(grad * student, axis=1, keepdims=True) * inv
        dg_hi, dg_lo = hi_lo(dg)
        zero = jnp.zeros_like(dg)
        g_key = jnp.where(lane == 0, dg_hi, jnp.where(lane == HALF, dg_lo, zero)).astype(BF16)
        g_later = jnp.where(lane < HALF, dg_hi, dg_lo).astype(BF16)
        g_norm = jnp.where(
            (lane == 0) | (lane == HALF), dg_hi, jnp.where(lane == 1, dg_lo, zero)
        ).astype(BF16)
        coupling = dot_nt(jnp.concatenate([numer_low, g_key], axis=1), v_pick)
        coupling = jnp.where(causal, coupling, 0.0).astype(BF16)
        later[...] += dot_tn(phi, jnp.concatenate([numer_low, g_later], axis=1))
        own_dphi[...] += dot_tn(phi, coupling)
        dphi = dot_nt(coupling, kphi_own)
        dphi = dphi + dot_nt(jnp.concatenate([numer_low, g_norm], axis=1), low[...])
        dl = pair_backward(pn, dphi).astype(BF16)
        q = qs[rows, :]
        ga, gb = dot_tn(q[:T], dl[:T]), dot_tn(q[T:], dl[T:])
        both = jnp.where(lane_d < HALF, ga, -gb).astype(BF16).reshape(SIDE, 16, D)
        parts[:, :, pl.ds(pl.multiple_of(j * D, D), D)] = both
        return carry

    lax.fori_loop(0, TILES, finish, 0)

    def exchange(n, source, target, me, to):
        def make(j):
            return pltpu.make_async_remote_copy(
                src_ref=source(j), dst_ref=target.at[me], send_sem=out_sem.at[n, j],
                recv_sem=in_sem.at[n, me], device_id=to(j), device_id_type=MESH,
            )

        def gather(own):
            total = own
            for j in NEAR:
                slot = (me + j) % SIDE
                pltpu.make_async_remote_copy(
                    src_ref=source(j), dst_ref=target.at[slot], send_sem=out_sem.at[n, j],
                    recv_sem=in_sem.at[n, slot], device_id=to(j), device_id_type=MESH,
                ).wait_recv()
                if own is not None:
                    total = total + target[slot].astype(F32)
            return total

        for j in FAR:
            make(j).start()

        def finished():
            for j in NEAR:
                make(j).wait_send()

        return gather, finished

    q_one, q_one_end = exchange(0, lambda j: parts.at[(f + j) % SIDE], got1, f, f_rank)

    norm = later[:, D:]
    norm_hi, norm_lo = hi_lo(norm + pltpu.roll(norm, HALF, 1))
    low[...] = jnp.concatenate(
        [later[:, :D], jnp.where(lane_d < HALF, norm_hi, norm_lo)], axis=1
    ).astype(BF16)
    kg_acc[...] = dot(pair_backward_t(e_own, g_own, own_dphi[...]).astype(BF16), k_own)
    lane_c = lanes(CHUNK)
    pick_c = jnp.where((lane_c == 0) | (lane_c == HALF), 1.0, 0.0).astype(BF16)

    def back(ss, carry):
        @pl.when(active(ss))
        def _():
            k, v = chunk_kv(ss)
            d = dot_nt(low[...], jnp.concatenate([v, pick_c], axis=1))
            kg_acc[...] += dot(
                pair_backward_t(kpn[ss, :HALF], kpn[ss, HALF:], d).astype(BF16), k
            )

        return carry

    lax.fori_loop(0, SIDE, back, 0)
    row = lax.broadcasted_iota(jnp.int32, (8, D), 0)

    def extra(value):
        hi, lo = hi_lo(value)
        return jnp.where(row == 0, hi, jnp.where(row == 1, lo, 0.0))

    def value_of(total):
        return total[8:9, 0:1] + total[9:10, 0:1]

    tail = extra(jnp.sum(loss_acc[...], keepdims=True).reshape(1, 1))
    for i in range(SIDE):
        kparts[i] = jnp.concatenate([kg_acc[pl.ds(8 * i, 8), :], tail], axis=0).astype(BF16)
    k_one, k_one_end = exchange(1, lambda j: kparts.at[(f + j) % SIDE], kgot1, f, f_rank)
    mid[...] = q_one(parts[f].astype(F32)).astype(BF16)
    q_two, q_two_end = exchange(2, lambda j: mid, got2, s, s_rank)
    total = k_one(kparts[f].astype(F32))
    kmid[...] = jnp.concatenate([total[:8], extra(value_of(total))], axis=0).astype(BF16)
    k_two, k_two_end = exchange(3, lambda j: kmid, kgot2, s, s_rank)
    full[...] = q_two(mid[...].astype(F32)).astype(BF16)
    q_three, q_three_end = exchange(4, lambda j: full, got3, f, f_rank)
    total = k_two(kmid[...].astype(F32))
    kfull[...] = total.astype(BF16)
    k_three, k_three_end = exchange(5, lambda j: kfull, kgot3, f, f_rank)
    mine[...] = jnp.broadcast_to(value_of(total), (8, D))
    h_one, h_one_end = exchange(6, lambda j: mine, got_loss, head, h_rank)
    got3[f] = full[...]
    kgot3[f] = kfull[...]
    q_three(None)
    qg_ref[...] = got3[...]
    k_three(None)
    kg_ref[...] = kgot3[...]
    loss_ref[...] = h_one(mine[...])
    for end in (q_one_end, k_one_end, q_two_end, k_two_end, q_three_end, k_three_end, h_one_end):
        end()
    for send in SENDS:
        copy(send).wait_send()


def unpack_kernel(student_ref, qg_ref, kg_ref, loss_ref, so_ref, qo_ref, ko_ref, lo_ref):
    so_ref[...] = student_ref[...]
    qo_ref[...] = qg_ref[...].reshape(D, GROUP * HALF).astype(F32)
    for i in range(SIDE):
        ko_ref[pl.ds(8 * i, 8), :] = kg_ref[i].astype(F32)[:8]
    lo_ref[...] = loss_ref[0:1, 0:1] * (1.0 / TOKENS)


def attend(queries, key_matrix, value_matrix, query_feature_weight, key_feature_weight):
    vmem = pl.BlockSpec(memory_space=pltpu.VMEM)
    anywhere = pl.BlockSpec(memory_space=pl.ANY)
    dma = pltpu.SemaphoreType.DMA
    one, all_of = (16,), (SIDE, 16)
    exchanges = (all_of, all_of, one, all_of, one, all_of)
    return pl.pallas_call(
        main_kernel,
        out_shape=(
            jax.ShapeDtypeStruct((T, GROUP * D), BF16),
            jax.ShapeDtypeStruct((SIDE, 16, GROUP * HALF), BF16),
            jax.ShapeDtypeStruct((SIDE, 16, D), BF16),
            jax.ShapeDtypeStruct((8, D), F32),
        ),
        in_specs=[vmem, anywhere, anywhere, vmem, vmem],
        out_specs=(vmem, vmem, vmem, vmem),
        scratch_shapes=[
            pltpu.VMEM((BLOCKS, 2 * T, D), BF16),
            pltpu.VMEM((ROWS, D), BF16),
            pltpu.VMEM((ROWS, D), F32),
            pltpu.VMEM((SIDE, D, CHUNK), F32),
            pltpu.VMEM((ROWS, D), F32),
            pltpu.VMEM((ROWS, 2 * D), F32),
            pltpu.VMEM((2, PAIR, CHUNK), F32),
            pltpu.VMEM((2, PAIR, CHUNK), BF16),
            pltpu.VMEM((SIDE, 1, CHUNK), F32),
            pltpu.VMEM((D, 2 * D), F32),
            pltpu.VMEM((D, 2 * D), F32),
            pltpu.VMEM((D, 2 * D), BF16),
            pltpu.VMEM((D, T), F32),
            pltpu.VMEM((8, D), F32),
            pltpu.VMEM((HALF, D), F32),
        ]
        + [pltpu.VMEM(shape + (512,), BF16) for shape in exchanges]
        + [pltpu.VMEM(shape + (D,), BF16) for shape in exchanges]
        + [
            pltpu.VMEM((8, D), F32),
            pltpu.VMEM((SIDE, 8, D), F32),
            dma((2,)),
            dma((BLOCKS,)),
            dma((len(SENDS),)),
            dma((7, SIDE)),
            dma((7, SIDE)),
        ],
        compiler_params=pltpu.CompilerParams(
            collective_id=0, has_side_effects=True, vmem_limit_bytes=56 * 1024 * 1024
        ),
        name="attend",
    )(queries, key_matrix, value_matrix, query_feature_weight, key_feature_weight.T)


def unpack(*operands):
    vmem = pl.BlockSpec(memory_space=pltpu.VMEM)
    return pl.pallas_call(
        unpack_kernel,
        out_shape=(
            jax.ShapeDtypeStruct((T, GROUP * D), BF16),
            jax.ShapeDtypeStruct((D, GROUP * HALF), F32),
            jax.ShapeDtypeStruct((HALF, D), F32),
            jax.ShapeDtypeStruct((1, 1), F32),
        ),
        in_specs=[vmem] * 4,
        out_specs=(vmem,) * 4,
        name="unpack",
    )(*operands)


def local(*operands):
    student, qo, ko, lo = unpack(*attend(*operands))
    return student, qo, ko.T, lo.reshape(())


def solution(mesh):
    placed = (
        P("seq", "head"),
        P("seq", "head"),
        P("seq", "head"),
        P(None, "head"),
        P(None, "head"),
    )
    return jax.shard_map(
        local,
        mesh=mesh,
        in_specs=placed,
        out_specs=(P("seq", "head"), P(None, "head"), P(None, "head"), P()),
        check_vma=False,
    )
```

time: 96.3 us -> 82.8 us (0.86)
  Pallas kernels: 90.1 us -> 81.9 us
  local copies, waits for them, and re-layouts: 5.05 us -> 0 us
    pallas_call x1, Pallas kernels: 37 us -> 1.87 us  [unpack(): pl.pallas_call(unpack_kernel, out_shape=(jax.ShapeDtypeStruct((T, GROUP *...]
    pallas_call x1, Pallas kernels: 53.1 us -> 80.1 us  [attend(): pl.pallas_call(main_kernel, out_shape=(jax.ShapeDtypeStruct((T, GROUP * D...]
    unnamed x10 -> x0, local copies, waits for them, and re-layouts: 3.87 us -> none
    slice x1 -> x0, local copies, waits for them, and re-layouts: 1.19 us -> none  [local(): return (student, qo, ko.T, lo[0, 0])]
where the time goes in v3:
time: 82.8 us; the launch traced here: 82.6 us
  Pallas kernels  81.9 us (99%)
    pallas_call x1, Pallas kernels, attend(): pl.pallas_call(main_kernel, out_shape=(jax.ShapeDtypeStruct((T, GROUP * D...  80.1 us
    pallas_call x1, Pallas kernels, unpack(): pl.pallas_call(unpack_kernel, out_shape=(jax.ShapeDtypeStruct((T, GROUP *...  1.87 us

profile of v3, /device:TPU:1, one launch (start us, length us, event | category | flops | bytes accessed | tf_op | source)
XLA Modules:
  0.0 82.6 jit_solution(5547638049805023129)
XLA Ops:
  0.6 80.1 %attend.1 = (bf16[144,1024]{1,0:T(8,128)(2,1)}, bf16[8,16,512]{2,1,0:T(8,128)(2,1)}, bf16[8,16,128]{2,1,0:T(8,128)(2,1)}, f32[8,128]{1,0:T(8,128)}) custom-call(bf16[144,1024]{1,0:T(8,128)(2,1)} %q_ref.1, bf16[144,128]{1,0:T(8,128)(2,1)} %k_hbm.1, bf16[144,128]{1,0:T(8,128)(2,1)} %v_hbm.1, bf16[128,512]{1,0:T(8,128)(2,1)} %wq_ref.1, bf16[64,128]{1,0:T(8,128)(2,1)} %bitcast.3), custom_call_target="tpu_custom_call" | custom-call | tf_op jit(solution)/shard_map/attend/pallas_call | solution.py:489
  80.7 1.9 %unpack.1 = (bf16[144,1024]{1,0:T(8,128)(2,1)}, f32[128,512]{1,0:T(8,128)}, f32[64,128]{1,0:T(8,128)}, f32[1,1]{1,0:T(1,128)}) custom-call(bf16[144,1024]{1,0:T(8,128)(2,1)} %get-tuple-element.12.student_ref, bf16[8,16,512]{2,1,0:T(8,128)(2,1)} %get-tuple-element.13.qg_ref, bf16[8,16,128]{2,1,0:T(8,128)(2,1)} %get-tuple-element.14.kg_ref, ...), custom_call_target="tpu_custom_call" | custom-call | tf_op jit(solution)/shard_map/unpack/pallas_call | solution.py:536

commit v4 on v3

--- a/solution.py
+++ b/solution.py
@@ -102,36 +102,29 @@
 NEAR = FAR[::-1]
 
 
-def plan():
-    waves = [[("own", 0, 0, 0)]]
-    for w in range(1, 9):
-        wave = []
-        if w <= 4:
-            wave.append(("f", 0, 0, 2 * w - 1))
-        if w <= 3:
-            wave.append(("f", 1, 0, 2 * w))
-        for h in range(1, 5):
-            d = w - h
-            if not 0 <= d <= 4:
-                continue
-            for k in (2 * d - 1, 2 * d) if 1 <= d <= 3 else ((0,) if d == 0 else (7,)):
-                if h <= 3 or k < 4:
-                    wave.append(("s", 0, h, k))
-                if h <= 3 or k >= 4:
-                    wave.append(("s", 1, h, k))
-        waves.append(wave)
-    return waves
-
-
-WAVES = plan()
+ARRIVAL = (
+    0, 10, 1, 110, 2, 20, 3, 111, 4, 11, 120, 12, 112, 30, 5, 113,
+    6, 13, 121, 14, 114, 130, 21, 122, 7, 22, 115, 40, 123, 15, 116, 16,
+    131, 23, 124, 24, 132, 31, 117, 17, 125, 32, 133, 25, 126, 26, 134, 33,
+    127, 34, 135, 41, 136, 27, 144, 42, 137, 35, 145, 36, 146, 43, 147, 37,
+)
+
+
+def unpacked(code):
+    way, hops, k = code // 100, code // 10 % 10, code % 10
+    if hops:
+        return ("s", way, hops, k)
+    return ("own", 0, 0, 0) if k == 0 else ("f", 1 - k % 2, 0, k)
+
+
+FLAT = [unpacked(code) for code in ARRIVAL]
 SLOT = {}
 SHIFT = []
-for item in (item for wave in WAVES for item in wave):
-    ring, way, hops, k = item
+for ring, way, hops, k in FLAT:
     SLOT[(0, 0, k) if hops == 0 else (way, hops, k)] = len(SHIFT)
-    SHIFT.append((-hops if way == 0 else hops, offset(k)))
-FLAT = [item for wave in WAVES for item in wave]
-BEFORE = [FLAT[a:b] for a, b in ((5, 13), (13, 25), (25, 32), (32, 39), (39, 45), (45, 51), (51, 59), (59, 64))]
+    SHIFT.append((-hops if way == 0 else hops, offset(k)) if hops else (0, offset(k)))
+CUTS = (9, 13, 25, 32, 39, 45, 51, 59, 64)
+BEFORE = [FLAT[a:b] for a, b in zip(CUTS, CUTS[1:])]
 
 
 def sends_after(item):
@@ -157,10 +150,11 @@
 
 
 def main_kernel(
-    q_ref, k_hbm, v_hbm, wq_ref, wk_ref,
-    student_ref, qg_ref, kg_ref, loss_ref,
+    q_hbm, k_hbm, v_hbm, wq_hbm, wk_hbm,
+    student_hbm, qg_ref, kg_ref, loss_ref,
     kv, qs, qpn, kpn, run_max, acc, scores, probs, bias_all, prefix, later, low, own_dphi, loss_acc, kg_acc,
     parts, got1, mid, got2, full, got3, kparts, kgot1, kmid, kgot2, kfull, kgot3, mine, got_loss,
+    phi_t, q_t, near_n, near_d, q_ref, wq_ref, wk_ref, student_ref,
     local_sem, recv_sem, send_sem, out_sem, in_sem,
 ):
     seq, head, f, s, stride_f, stride_s = place()
@@ -175,6 +169,12 @@
     load_v = pltpu.make_async_copy(v_hbm, kv.at[0, pl.ds(T, T)], local_sem.at[1])
     load_k.start()
     load_v.start()
+    rest = [
+        pltpu.make_async_copy(source, target, local_sem.at[n])
+        for n, source, target in ((2, wk_hbm, wk_ref), (3, q_hbm, q_ref), (4, wq_hbm, wq_ref))
+    ]
+    for load in rest:
+        load.start()
     def f_rank(j):
         return rank((f + j) % SIDE, s)
 
@@ -232,6 +232,9 @@
         bias_all[n] = row
         on.append(count)
 
+    for load in rest:
+        load.wait()
+
     def active(ci):
         return sum(jnp.where(ci == n, on[n], 0) for n in range(SIDE)) > 0
 
@@ -251,10 +254,8 @@
     loss_acc[...] = jnp.zeros_like(loss_acc)
 
     def first(j, carry):
-        @pl.when(j == 3)
-        def _():
-            relay(FLAT[1:5])
-
+        pl.when(j == 2)(functools.partial(relay, FLAT[1:5]))
+        pl.when(j == 3)(functools.partial(relay, FLAT[5:9]))
         rows = pl.ds(pl.multiple_of(j * PAIR, PAIR), PAIR)
         q_a = q_ref[:, pl.ds(pl.multiple_of(j * 2 * D, D), D)]
         q_b = q_ref[:, pl.ds(pl.multiple_of(j * 2 * D + D, D), D)]
@@ -265,7 +266,15 @@
         plus = lanes(T) < HALF
         xa = jnp.where(plus, la, -pltpu.roll(la, HALF, 1))
         xb = jnp.where(plus, pltpu.roll(lb, HALF, 1), -lb)
-        qpn[rows, :] = feature_pair(jnp.concatenate([xa, xb], axis=0))
+        pn = feature_pair(jnp.concatenate([xa, xb], axis=0))
+        qpn[rows, :] = pn
+        phi = pn.astype(BF16)
+        phi_t[j] = phi.T
+        q_t[2 * j] = q_a.T
+        q_t[2 * j + 1] = q_b.T
+        intra = jnp.where(causal, dot(phi, kphi_own), 0.0)
+        near_n[rows, :] = dot(intra.astype(BF16), v_own)
+        near_d[rows, :] = jnp.broadcast_to(jnp.sum(intra, axis=1, keepdims=True), (PAIR, D))
         scores = jnp.where(causal, dot_nt(q, k_own) * SCALE2, NEG)
         top = jnp.max(scores, axis=1, keepdims=True)
         p = jnp.exp2(scores - top).astype(BF16)
@@ -286,7 +295,13 @@
         for n in range(SIDE):
             pl.when(ci == n)(functools.partial(relay, BEFORE[n]))
 
-        @pl.when(active(ci))
+        live = active(ci)
+
+        @pl.when(jnp.logical_not(live))
+        def _():
+            kpn[ci] = jnp.zeros((D, CHUNK), F32)
+
+        @pl.when(live)
         def _():
             k, v = chunk_kv(ci)
             v1 = jnp.concatenate([v, jnp.ones((CHUNK, D), BF16)], axis=1)
@@ -340,15 +355,50 @@
     pick_t = jnp.where((lane_t == 0) | (lane_t == HALF), 1.0, 0.0).astype(BF16)
     v_pick = jnp.concatenate([v_own, pick_t], axis=1)
 
-    def finish(j, carry):
+    def exchange(n, source, target, me, to):
+        def make(j):
+            return pltpu.make_async_remote_copy(
+                src_ref=source(j), dst_ref=target.at[me], send_sem=out_sem.at[n, j],
+                recv_sem=in_sem.at[n, me], device_id=to(j), device_id_type=MESH,
+            )
+
+        def gather(own):
+            total = own
+            for j in NEAR:
+                slot = (me + j) % SIDE
+                pltpu.make_async_remote_copy(
+                    src_ref=source(j), dst_ref=target.at[slot], send_sem=out_sem.at[n, j],
+                    recv_sem=in_sem.at[n, slot], device_id=to(j), device_id_type=MESH,
+                ).wait_recv()
+                if own is not None:
+                    total = total + target[slot].astype(F32)
+            return total
+
+        def begin():
+            for j in FAR:
+                make(j).start()
+
+        def finished():
+            for j in NEAR:
+                make(j).wait_send()
+
+        return begin, gather, finished
+
+    def tile_exchange(r):
+        return exchange(r, lambda j: parts.at[r, (f + j) % SIDE], got1.at[r], f, f_rank)
+
+    tiles = [tile_exchange(r) for r in range(TILES)]
+
+    def finish(j):
+        if j:
+            tiles[j - 1][0]()
         rows = pl.ds(pl.multiple_of(j * PAIR, PAIR), PAIR)
         pn = qpn[rows, :]
         phi = pn.astype(BF16)
-        intra = jnp.where(causal, dot(phi, kphi_own), 0.0)
         far = dot(phi, low[...])
-        numer = dot(intra.astype(BF16), v_own) + far[:, :D]
+        numer = near_n[rows, :] + far[:, :D]
         far_d = far[:, D:]
-        denom = jnp.sum(intra, axis=1, keepdims=True) + (far_d + pltpu.roll(far_d, HALF, 1))
+        denom = near_d[rows, :] + (far_d + pltpu.roll(far_d, HALF, 1))
         inv = 1.0 / denom
         student = numer * inv
         student_low = student.astype(BF16)
@@ -370,70 +420,37 @@
         ).astype(BF16)
         coupling = dot_nt(jnp.concatenate([numer_low, g_key], axis=1), v_pick)
         coupling = jnp.where(causal, coupling, 0.0).astype(BF16)
-        later[...] += dot_tn(phi, jnp.concatenate([numer_low, g_later], axis=1))
-        own_dphi[...] += dot_tn(phi, coupling)
+        later[...] += dot(phi_t[j], jnp.concatenate([numer_low, g_later], axis=1))
+        own_dphi[...] += dot(phi_t[j], coupling)
         dphi = dot_nt(coupling, kphi_own)
         dphi = dphi + dot_nt(jnp.concatenate([numer_low, g_norm], axis=1), low[...])
         dl = pair_backward(pn, dphi).astype(BF16)
-        q = qs[rows, :]
-        ga, gb = dot_tn(q[:T], dl[:T]), dot_tn(q[T:], dl[T:])
+        ga, gb = dot(q_t[2 * j], dl[:T]), dot(q_t[2 * j + 1], dl[T:])
         both = jnp.where(lane_d < HALF, ga, -gb).astype(BF16).reshape(SIDE, 16, D)
-        parts[:, :, pl.ds(pl.multiple_of(j * D, D), D)] = both
-        return carry
-
-    lax.fori_loop(0, TILES, finish, 0)
-
-    def exchange(n, source, target, me, to):
-        def make(j):
-            return pltpu.make_async_remote_copy(
-                src_ref=source(j), dst_ref=target.at[me], send_sem=out_sem.at[n, j],
-                recv_sem=in_sem.at[n, me], device_id=to(j), device_id_type=MESH,
-            )
-
-        def gather(own):
-            total = own
-            for j in NEAR:
-                slot = (me + j) % SIDE
-                pltpu.make_async_remote_copy(
-                    src_ref=source(j), dst_ref=target.at[slot], send_sem=out_sem.at[n, j],
-                    recv_sem=in_sem.at[n, slot], device_id=to(j), device_id_type=MESH,
-                ).wait_recv()
-                if own is not None:
-                    total = total + target[slot].astype(F32)
-            return total
-
-        for j in FAR:
-            make(j).start()
-
-        def finished():
-            for j in NEAR:
-                make(j).wait_send()
-
-        return gather, finished
-
-    q_one, q_one_end = exchange(0, lambda j: parts.at[(f + j) % SIDE], got1, f, f_rank)
+        parts[j] = both
+
+    for j in range(TILES):
+        finish(j)
+    put = pltpu.make_async_copy(student_ref, student_hbm, local_sem.at[5])
 
     norm = later[:, D:]
     norm_hi, norm_lo = hi_lo(norm + pltpu.roll(norm, HALF, 1))
     low[...] = jnp.concatenate(
         [later[:, :D], jnp.where(lane_d < HALF, norm_hi, norm_lo)], axis=1
     ).astype(BF16)
+    tiles[TILES - 1][0]()
+    put.start()
     kg_acc[...] = dot(pair_backward_t(e_own, g_own, own_dphi[...]).astype(BF16), k_own)
     lane_c = lanes(CHUNK)
     pick_c = jnp.where((lane_c == 0) | (lane_c == HALF), 1.0, 0.0).astype(BF16)
 
     def back(ss, carry):
-        @pl.when(active(ss))
-        def _():
-            k, v = chunk_kv(ss)
-            d = dot_nt(low[...], jnp.concatenate([v, pick_c], axis=1))
-            kg_acc[...] += dot(
-                pair_backward_t(kpn[ss, :HALF], kpn[ss, HALF:], d).astype(BF16), k
-            )
-
+        k, v = chunk_kv(ss)
+        d = dot_nt(low[...], jnp.concatenate([v, pick_c], axis=1))
+        kg_acc[...] += dot(pair_backward_t(kpn[ss, :HALF], kpn[ss, HALF:], d).astype(BF16), k)
         return carry
 
-    lax.fori_loop(0, SIDE, back, 0)
+    lax.fori_loop(0, SIDE, back, 0, unroll=True)
     row = lax.broadcasted_iota(jnp.int32, (8, D), 0)
 
     def extra(value):
@@ -446,30 +463,45 @@
     tail = extra(jnp.sum(loss_acc[...], keepdims=True).reshape(1, 1))
     for i in range(SIDE):
         kparts[i] = jnp.concatenate([kg_acc[pl.ds(8 * i, 8), :], tail], axis=0).astype(BF16)
-    k_one, k_one_end = exchange(1, lambda j: kparts.at[(f + j) % SIDE], kgot1, f, f_rank)
-    mid[...] = q_one(parts[f].astype(F32)).astype(BF16)
-    q_two, q_two_end = exchange(2, lambda j: mid, got2, s, s_rank)
+    k_begin, k_one, k_one_end = exchange(
+        4, lambda j: kparts.at[(f + j) % SIDE], kgot1, f, f_rank
+    )
+    k_begin()
+    for send in SENDS:
+        copy(send).wait_send()
+    for r in range(TILES):
+        mid[:, pl.ds(r * D, D)] = tiles[r][1](parts[r, f].astype(F32)).astype(BF16)
+    begin, q_two, q_two_end = exchange(5, lambda j: mid, got2, s, s_rank)
+    begin()
     total = k_one(kparts[f].astype(F32))
     kmid[...] = jnp.concatenate([total[:8], extra(value_of(total))], axis=0).astype(BF16)
-    k_two, k_two_end = exchange(3, lambda j: kmid, kgot2, s, s_rank)
+    begin, k_two, k_two_end = exchange(6, lambda j: kmid, kgot2, s, s_rank)
+    begin()
+    for tile in tiles:
+        tile[2]()
+    k_one_end()
+    put.wait()
     full[...] = q_two(mid[...].astype(F32)).astype(BF16)
-    q_three, q_three_end = exchange(4, lambda j: full, got3, f, f_rank)
+    begin, q_three, q_three_end = exchange(7, lambda j: full, got3, f, f_rank)
+    begin()
     total = k_two(kmid[...].astype(F32))
     kfull[...] = total.astype(BF16)
-    k_three, k_three_end = exchange(5, lambda j: kfull, kgot3, f, f_rank)
+    begin, k_three, k_three_end = exchange(8, lambda j: kfull, kgot3, f, f_rank)
+    begin()
     mine[...] = jnp.broadcast_to(value_of(total), (8, D))
-    h_one, h_one_end = exchange(6, lambda j: mine, got_loss, head, h_rank)
+    begin, h_one, h_one_end = exchange(9, lambda j: mine, got_loss, head, h_rank)
+    begin()
     got3[f] = full[...]
     kgot3[f] = kfull[...]
+    q_two_end()
+    k_two_end()
     q_three(None)
     qg_ref[...] = got3[...]
     k_three(None)
     kg_ref[...] = kgot3[...]
     loss_ref[...] = h_one(mine[...])
-    for end in (q_one_end, k_one_end, q_two_end, k_two_end, q_three_end, k_three_end, h_one_end):
+    for end in (q_three_end, k_three_end, h_one_end):
         end()
-    for send in SENDS:
-        copy(send).wait_send()
 
 
 def unpack_kernel(student_ref, qg_ref, kg_ref, loss_ref, so_ref, qo_ref, ko_ref, lo_ref):
@@ -494,8 +526,8 @@
             jax.ShapeDtypeStruct((SIDE, 16, D), BF16),
             jax.ShapeDtypeStruct((8, D), F32),
         ),
-        in_specs=[vmem, anywhere, anywhere, vmem, vmem],
-        out_specs=(vmem, vmem, vmem, vmem),
+        in_specs=[anywhere] * 5,
+        out_specs=(anywhere, vmem, vmem, vmem),
         scratch_shapes=[
             pltpu.VMEM((BLOCKS, 2 * T, D), BF16),
             pltpu.VMEM((ROWS, D), BF16),
@@ -513,16 +545,25 @@
             pltpu.VMEM((8, D), F32),
             pltpu.VMEM((HALF, D), F32),
         ]
-        + [pltpu.VMEM(shape + (512,), BF16) for shape in exchanges]
+        + [pltpu.VMEM((TILES,) + all_of + (D,), BF16)] * 2
+        + [pltpu.VMEM(shape + (512,), BF16) for shape in exchanges[2:]]
         + [pltpu.VMEM(shape + (D,), BF16) for shape in exchanges]
         + [
             pltpu.VMEM((8, D), F32),
             pltpu.VMEM((SIDE, 8, D), F32),
-            dma((2,)),
+            pltpu.VMEM((TILES, D, PAIR), BF16),
+            pltpu.VMEM((GROUP, D, T), BF16),
+            pltpu.VMEM((ROWS, D), F32),
+            pltpu.VMEM((ROWS, D), F32),
+            pltpu.VMEM((T, GROUP * D), BF16),
+            pltpu.VMEM((D, GROUP * HALF), BF16),
+            pltpu.VMEM((HALF, D), BF16),
+            pltpu.VMEM((T, GROUP * D), BF16),
+            dma((6,)),
             dma((BLOCKS,)),
             dma((len(SENDS),)),
-            dma((7, SIDE)),
-            dma((7, SIDE)),
+            dma((10, SIDE)),
+            dma((10, SIDE)),
         ],
         compiler_params=pltpu.CompilerParams(
             collective_id=0, has_side_effects=True, vmem_limit_bytes=56 * 1024 * 1024

time: 82.8 us -> 79.5 us (0.960)
  Pallas kernels: 81.9 us -> 78.7 us
    pallas_call x1, Pallas kernels: 80.1 us -> 76.9 us  [attend(): pl.pallas_call(main_kernel, out_shape=(jax.ShapeDtypeStruct((T, GROUP * D...]
where the time goes in v4:
time: 79.5 us; the launch traced here: 79.4 us
  Pallas kernels  78.7 us (99%)
    pallas_call x1, Pallas kernels, attend(): pl.pallas_call(main_kernel, out_shape=(jax.ShapeDtypeStruct((T, GROUP * D...  76.9 us
    pallas_call x1, Pallas kernels, unpack(): pl.pallas_call(unpack_kernel, out_shape=(jax.ShapeDtypeStruct((T, GROUP *...  1.87 us

profile of v4, /device:TPU:1, one launch (start us, length us, event | category | flops | bytes accessed | tf_op | source)
XLA Modules:
  0.0 79.4 jit_solution(12812543110271815405)
XLA Ops:
  0.6 76.9 %attend.1 = (bf16[144,1024]{1,0:T(8,128)(2,1)}, bf16[8,16,512]{2,1,0:T(8,128)(2,1)}, bf16[8,16,128]{2,1,0:T(8,128)(2,1)}, f32[8,128]{1,0:T(8,128)}) custom-call(bf16[144,1024]{1,0:T(8,128)(2,1)} %q_hbm.1, bf16[144,128]{1,0:T(8,128)(2,1)} %k_hbm.1, bf16[144,128]{1,0:T(8,128)(2,1)} %v_hbm.1, bf16[128,512]{1,0:T(8,128)(2,1)} %wq_hbm.1, bf16[64,128]{1,0:T(8,128)(2,1)} %bitcast.3), custom_call_target="tpu_custom_call" | custom-call | tf_op jit(solution)/shard_map/attend/pallas_call | solution.py:521
  77.5 1.9 %unpack.1 = (bf16[144,1024]{1,0:T(8,128)(2,1)}, f32[128,512]{1,0:T(8,128)}, f32[64,128]{1,0:T(8,128)}, f32[1,1]{1,0:T(1,128)}) custom-call(bf16[144,1024]{1,0:T(8,128)(2,1)} %get-tuple-element.12.student_ref, bf16[8,16,512]{2,1,0:T(8,128)(2,1)} %get-tuple-element.13.qg_ref, bf16[8,16,128]{2,1,0:T(8,128)(2,1)} %get-tuple-element.14.kg_ref, ...), custom_call_target="tpu_custom_call" | custom-call | tf_op jit(solution)/shard_map/unpack/pallas_call | solution.py:577

commit v5 on v4

--- a/solution.py
+++ b/solution.py
@@ -291,8 +291,51 @@
         v = kv[pl.ds(base, SIDE), pl.ds(T, T), :].reshape(CHUNK, D)
         return k, v
 
+    def work(ci, ready=None, finish=None):
+        k, v = chunk_kv(ci)
+        v1 = jnp.concatenate([v, jnp.ones((CHUNK, D), BF16)], axis=1)
+        bias = bias_all[ci]
+        seen = bias == 0.0
+        cuts = [(i, min(256, CHUNK - i)) for i in range(0, CHUNK, 256)]
+
+        def score(r):
+            rows = pl.ds(r * PAIR, PAIR)
+            q = qs[rows, :]
+            top = None
+            for i, n in cuts:
+                x = dot_nt(q, k[i:i + n]) * SCALE2 + bias[:, i:i + n]
+                scores[r % 2, :, pl.ds(i, n)] = x
+                for c in range(0, n, D):
+                    top = x[:, c:c + D] if top is None else jnp.maximum(top, x[:, c:c + D])
+            old = run_max[rows, :]
+            new = jnp.maximum(old, jnp.max(top, axis=1, keepdims=True))
+            run_max[rows, :] = new
+            return new, jnp.exp2(old - new)
+
+        def weigh(r, new, alpha):
+            rows = pl.ds(r * PAIR, PAIR)
+            for i in range(0, CHUNK, D):
+                x = scores[r % 2, :, pl.ds(i, D)]
+                probs[r % 2, :, pl.ds(i, D)] = jnp.exp2(x - new).astype(BF16)
+            out = dot(probs[r % 2], v1)
+            acc[rows, :] = acc[rows, :] * jnp.concatenate([alpha, alpha], axis=1) + out
+
+        held = score(0)
+        e, g = feature_pair_t(dot_nt(wk_ref[...], k))
+        pn = jnp.where(seen, jnp.concatenate([e, g], axis=0), 0.0)
+        kpn[ci] = pn
+        prefix[...] += dot(pn.astype(BF16), v1)
+        if ready is not None:
+            ready()
+        for r in range(TILES):
+            ahead = score(r + 1) if r + 1 < TILES else None
+            weigh(r, *held)
+            if finish is not None:
+                finish(r)
+            held = ahead
+
     def step(ci, carry):
-        for n in range(SIDE):
+        for n in range(SIDE - 1):
             pl.when(ci == n)(functools.partial(relay, BEFORE[n]))
 
         live = active(ci)
@@ -301,55 +344,18 @@
         def _():
             kpn[ci] = jnp.zeros((D, CHUNK), F32)
 
-        @pl.when(live)
-        def _():
-            k, v = chunk_kv(ci)
-            v1 = jnp.concatenate([v, jnp.ones((CHUNK, D), BF16)], axis=1)
-            bias = bias_all[ci]
-            seen = bias == 0.0
-            cuts = [(i, min(256, CHUNK - i)) for i in range(0, CHUNK, 256)]
-
-            def score(r):
-                rows = pl.ds(r * PAIR, PAIR)
-                q = qs[rows, :]
-                top = None
-                for i, n in cuts:
-                    x = dot_nt(q, k[i:i + n]) * SCALE2 + bias[:, i:i + n]
-                    scores[r % 2, :, pl.ds(i, n)] = x
-                    for c in range(0, n, D):
-                        top = x[:, c:c + D] if top is None else jnp.maximum(top, x[:, c:c + D])
-                old = run_max[rows, :]
-                new = jnp.maximum(old, jnp.max(top, axis=1, keepdims=True))
-                run_max[rows, :] = new
-                return new, jnp.exp2(old - new)
-
-            def weigh(r, new, alpha):
-                rows = pl.ds(r * PAIR, PAIR)
-                for i in range(0, CHUNK, D):
-                    x = scores[r % 2, :, pl.ds(i, D)]
-                    probs[r % 2, :, pl.ds(i, D)] = jnp.exp2(x - new).astype(BF16)
-                out = dot(probs[r % 2], v1)
-                acc[rows, :] = acc[rows, :] * jnp.concatenate([alpha, alpha], axis=1) + out
-
-            held = score(0)
-            e, g = feature_pair_t(dot_nt(wk_ref[...], k))
-            pn = jnp.where(seen, jnp.concatenate([e, g], axis=0), 0.0)
-            kpn[ci] = pn
-            prefix[...] += dot(pn.astype(BF16), v1)
-            for r in range(TILES):
-                ahead = score(r + 1) if r + 1 < TILES else None
-                weigh(r, *held)
-                held = ahead
-
+        pl.when(live)(functools.partial(work, ci))
         return carry
 
-    lax.fori_loop(0, SIDE, step, 0)
+    lax.fori_loop(0, SIDE - 1, step, 0)
 
     lane_d = lanes(D)
-    norm_hi, norm_lo = hi_lo(prefix[:, D:])
-    low[...] = jnp.concatenate(
-        [prefix[:, :D], jnp.where(lane_d < HALF, norm_hi, norm_lo)], axis=1
-    ).astype(BF16)
+    def ready():
+        norm_hi, norm_lo = hi_lo(prefix[:, D:])
+        low[...] = jnp.concatenate(
+            [prefix[:, :D], jnp.where(lane_d < HALF, norm_hi, norm_lo)], axis=1
+        ).astype(BF16)
+
     lane = lanes(PAIR)
     lane_t = lanes(T)
     pick_t = jnp.where((lane_t == 0) | (lane_t == HALF), 1.0, 0.0).astype(BF16)
@@ -384,10 +390,18 @@
 
         return begin, gather, finished
 
-    def tile_exchange(r):
+    def tile_one(r):
         return exchange(r, lambda j: parts.at[r, (f + j) % SIDE], got1.at[r], f, f_rank)
 
-    tiles = [tile_exchange(r) for r in range(TILES)]
+    def tile_two(r):
+        return exchange(TILES + r, lambda j: mid.at[r], got2.at[r], s, s_rank)
+
+    def tile_three(r):
+        return exchange(2 * TILES + r, lambda j: full.at[r], got3.at[r], f, f_rank)
+
+    tiles = [tile_one(r) for r in range(TILES)]
+    twos = [tile_two(r) for r in range(TILES)]
+    threes = [tile_three(r) for r in range(TILES)]
 
     def finish(j):
         if j:
@@ -429,8 +443,8 @@
         both = jnp.where(lane_d < HALF, ga, -gb).astype(BF16).reshape(SIDE, 16, D)
         parts[j] = both
 
-    for j in range(TILES):
-        finish(j)
+    relay(BEFORE[SIDE - 1])
+    work(SIDE - 1, ready, finish)
     put = pltpu.make_async_copy(student_ref, student_hbm, local_sem.at[5])
 
     norm = later[:, D:]
@@ -464,49 +478,52 @@
     for i in range(SIDE):
         kparts[i] = jnp.concatenate([kg_acc[pl.ds(8 * i, 8), :], tail], axis=0).astype(BF16)
     k_begin, k_one, k_one_end = exchange(
-        4, lambda j: kparts.at[(f + j) % SIDE], kgot1, f, f_rank
+        12, lambda j: kparts.at[(f + j) % SIDE], kgot1, f, f_rank
     )
     k_begin()
+    for r in range(TILES):
+        mid[r] = tiles[r][1](parts[r, f].astype(F32)).astype(BF16)
+        twos[r][0]()
+    total = k_one(kparts[f].astype(F32))
+    kmid[...] = jnp.concatenate([total[:8], extra(value_of(total))], axis=0).astype(BF16)
+    begin, k_two, k_two_end = exchange(13, lambda j: kmid, kgot2, s, s_rank)
+    begin()
     for send in SENDS:
         copy(send).wait_send()
     for r in range(TILES):
-        mid[:, pl.ds(r * D, D)] = tiles[r][1](parts[r, f].astype(F32)).astype(BF16)
-    begin, q_two, q_two_end = exchange(5, lambda j: mid, got2, s, s_rank)
-    begin()
-    total = k_one(kparts[f].astype(F32))
-    kmid[...] = jnp.concatenate([total[:8], extra(value_of(total))], axis=0).astype(BF16)
-    begin, k_two, k_two_end = exchange(6, lambda j: kmid, kgot2, s, s_rank)
-    begin()
-    for tile in tiles:
-        tile[2]()
-    k_one_end()
-    put.wait()
-    full[...] = q_two(mid[...].astype(F32)).astype(BF16)
-    begin, q_three, q_three_end = exchange(7, lambda j: full, got3, f, f_rank)
-    begin()
+        full[r] = twos[r][1](mid[r].astype(F32)).astype(BF16)
+        threes[r][0]()
     total = k_two(kmid[...].astype(F32))
     kfull[...] = total.astype(BF16)
-    begin, k_three, k_three_end = exchange(8, lambda j: kfull, kgot3, f, f_rank)
+    begin, k_three, k_three_end = exchange(14, lambda j: kfull, kgot3, f, f_rank)
     begin()
     mine[...] = jnp.broadcast_to(value_of(total), (8, D))
-    begin, h_one, h_one_end = exchange(9, lambda j: mine, got_loss, head, h_rank)
+    begin, h_one, h_one_end = exchange(15, lambda j: mine, got_loss, head, h_rank)
     begin()
-    got3[f] = full[...]
+    put.wait()
+    for r in range(TILES):
+        got3[r, f] = full[r]
+        tiles[r][2]()
+        twos[r][2]()
     kgot3[f] = kfull[...]
-    q_two_end()
+    k_one_end()
     k_two_end()
-    q_three(None)
-    qg_ref[...] = got3[...]
+    for r in range(TILES):
+        threes[r][1](None)
+        qg_ref[r] = got3[r]
     k_three(None)
     kg_ref[...] = kgot3[...]
     loss_ref[...] = h_one(mine[...])
-    for end in (q_three_end, k_three_end, h_one_end):
-        end()
+    for r in range(TILES):
+        threes[r][2]()
+    k_three_end()
+    h_one_end()
 
 
 def unpack_kernel(student_ref, qg_ref, kg_ref, loss_ref, so_ref, qo_ref, ko_ref, lo_ref):
     so_ref[...] = student_ref[...]
-    qo_ref[...] = qg_ref[...].reshape(D, GROUP * HALF).astype(F32)
+    for r in range(TILES):
+        qo_ref[:, pl.ds(r * D, D)] = qg_ref[r].reshape(D, D).astype(F32)
     for i in range(SIDE):
         ko_ref[pl.ds(8 * i, 8), :] = kg_ref[i].astype(F32)[:8]
     lo_ref[...] = loss_ref[0:1, 0:1] * (1.0 / TOKENS)
@@ -522,7 +539,7 @@
         main_kernel,
         out_shape=(
             jax.ShapeDtypeStruct((T, GROUP * D), BF16),
-            jax.ShapeDtypeStruct((SIDE, 16, GROUP * HALF), BF16),
+            jax.ShapeDtypeStruct((TILES, SIDE, 16, D), BF16),
             jax.ShapeDtypeStruct((SIDE, 16, D), BF16),
             jax.ShapeDtypeStruct((8, D), F32),
         ),
@@ -545,8 +562,7 @@
             pltpu.VMEM((8, D), F32),
             pltpu.VMEM((HALF, D), F32),
         ]
-        + [pltpu.VMEM((TILES,) + all_of + (D,), BF16)] * 2
-        + [pltpu.VMEM(shape + (512,), BF16) for shape in exchanges[2:]]
+        + [pltpu.VMEM((TILES,) + shape + (D,), BF16) for shape in exchanges]
         + [pltpu.VMEM(shape + (D,), BF16) for shape in exchanges]
         + [
             pltpu.VMEM((8, D), F32),
@@ -562,8 +578,8 @@
             dma((6,)),
             dma((BLOCKS,)),
             dma((len(SENDS),)),
-            dma((10, SIDE)),
-            dma((10, SIDE)),
+            dma((16, SIDE)),
+            dma((16, SIDE)),
         ],
         compiler_params=pltpu.CompilerParams(
             collective_id=0, has_side_effects=True, vmem_limit_bytes=56 * 1024 * 1024

time: 79.5 us -> 80.4 us (1.011)
  Pallas kernels: 78.7 us -> 79.6 us
    pallas_call x1, Pallas kernels: 76.9 us -> 77.7 us  [attend(): pl.pallas_call(main_kernel, out_shape=(jax.ShapeDtypeStruct((T, GROUP * D...]
where the time goes in v5:
time: 80.4 us; the launch traced here: 80.2 us
  Pallas kernels  79.6 us (99%)
    pallas_call x1, Pallas kernels, attend(): pl.pallas_call(main_kernel, out_shape=(jax.ShapeDtypeStruct((T, GROUP * D...  77.7 us
    pallas_call x1, Pallas kernels, unpack(): pl.pallas_call(unpack_kernel, out_shape=(jax.ShapeDtypeStruct((T, GROUP *...  1.88 us

profile of v5, /device:TPU:1, one launch (start us, length us, event | category | flops | bytes accessed | tf_op | source)
XLA Modules:
  0.0 80.2 jit_solution(2045579831445401932)
XLA Ops:
  0.6 77.7 %attend.1 = (bf16[144,1024]{1,0:T(8,128)(2,1)}, bf16[4,8,16,128]{3,2,1,0:T(8,128)(2,1)}, bf16[8,16,128]{2,1,0:T(8,128)(2,1)}, f32[8,128]{1,0:T(8,128)}) custom-call(bf16[144,1024]{1,0:T(8,128)(2,1)} %q_hbm.1, bf16[144,128]{1,0:T(8,128)(2,1)} %k_hbm.1, bf16[144,128]{1,0:T(8,128)(2,1)} %v_hbm.1, bf16[128,512]{1,0:T(8,128)(2,1)} %wq_hbm.1, bf16[64,128]{1,0:T(8,128)(2,1)} %bitcast.3), custom_call_target="tpu_custom_call" | custom-call | tf_op jit(solution)/shard_map/attend/pallas_call | solution.py:538
  78.4 1.9 %unpack.1 = (bf16[144,1024]{1,0:T(8,128)(2,1)}, f32[128,512]{1,0:T(8,128)}, f32[64,128]{1,0:T(8,128)}, f32[1,1]{1,0:T(1,128)}) custom-call(bf16[144,1024]{1,0:T(8,128)(2,1)} %get-tuple-element.12.student_ref, bf16[4,8,16,128]{3,2,1,0:T(8,128)(2,1)} %get-tuple-element.13.qg_ref, bf16[8,16,128]{2,1,0:T(8,128)(2,1)} %get-tuple-element.14.kg_ref, ...), custom_call_target="tpu_custom_call" | custom-call | tf_op jit(solution)/shard_map/unpack/pallas_call | solution.py:593

commit v6 on v4

--- a/solution.py
+++ b/solution.py
@@ -14,7 +14,9 @@
 SIDE = 8
 BLOCKS = SIDE * SIDE
 TOKENS = BLOCKS * T
-CHUNK = SIDE * T
+SEVEN = 7
+CHUNKS = 9
+CHUNK = SEVEN * T
 ROWS = GROUP * T
 PAIR = 2 * T
 TILES = ROWS // PAIR
@@ -123,7 +125,7 @@
 for ring, way, hops, k in FLAT:
     SLOT[(0, 0, k) if hops == 0 else (way, hops, k)] = len(SHIFT)
     SHIFT.append((-hops if way == 0 else hops, offset(k)) if hops else (0, offset(k)))
-CUTS = (9, 13, 25, 32, 39, 45, 51, 59, 64)
+CUTS = (9, 12, 21, 29, 35, 41, 47, 53, 59, 64)
 BEFORE = [FLAT[a:b] for a, b in zip(CUTS, CUTS[1:])]
 
 
@@ -185,9 +187,12 @@
         return (seq, (head + j) % SIDE)
 
     barrier = pltpu.get_barrier_semaphore()
-    for to in (f_rank, s_rank, h_rank):
-        for j in range(1, SIDE):
-            pl.semaphore_signal(barrier, inc=1, device_id=to(j), device_id_type=MESH)
+    f_ring = [(None, f)] + [(f_rank(j), (f + j) % SIDE) for j in range(1, SIDE)]
+    s_ring = [(None, s)] + [(s_rank(j), (s + j) % SIDE) for j in range(1, SIDE)]
+    h_ring = [(None, head)] + [(h_rank(j), (head + j) % SIDE) for j in range(1, SIDE)]
+    for ring in (f_ring, s_ring, h_ring):
+        for peer, _ in ring[1:]:
+            pl.semaphore_signal(barrier, inc=1, device_id=peer, device_id_type=MESH)
     load_k.wait()
     load_v.wait()
     pl.semaphore_wait(barrier, 3 * (SIDE - 1))
@@ -220,11 +225,11 @@
 
     block = lax.broadcasted_iota(jnp.int32, (1, CHUNK), 1) // T
     on = []
-    for n in range(SIDE):
+    for n in range(CHUNKS):
         row = jnp.zeros((1, CHUNK), F32)
         count = 0
-        for j in range(SIDE):
-            ds, df = SHIFT[n * SIDE + j]
+        for j in range(SEVEN):
+            ds, df = SHIFT[1 + n * SEVEN + j]
             there = ((s + ds + SIDE) % SIDE) * stride_s + ((f + df + SIDE) % SIDE) * stride_f
             hidden = there >= seq
             row = jnp.where((block == j) & hidden, NEG, row)
@@ -236,7 +241,7 @@
         load.wait()
 
     def active(ci):
-        return sum(jnp.where(ci == n, on[n], 0) for n in range(SIDE)) > 0
+        return sum(jnp.where(ci == n, on[n], 0) for n in range(CHUNKS)) > 0
 
     k_own = kv[0, pl.ds(0, T), :]
     v_own = kv[0, pl.ds(T, T), :]
@@ -286,13 +291,13 @@
     lax.fori_loop(0, TILES, first, 0)
 
     def chunk_kv(ss):
-        base = pl.multiple_of(ss * SIDE, SIDE)
-        k = kv[pl.ds(base, SIDE), pl.ds(0, T), :].reshape(CHUNK, D)
-        v = kv[pl.ds(base, SIDE), pl.ds(T, T), :].reshape(CHUNK, D)
+        blocks = pl.ds(1 + ss * SEVEN, SEVEN)
+        k = kv[blocks, pl.ds(0, T), :].reshape(CHUNK, D)
+        v = kv[blocks, pl.ds(T, T), :].reshape(CHUNK, D)
         return k, v
 
     def step(ci, carry):
-        for n in range(SIDE):
+        for n in range(CHUNKS):
             pl.when(ci == n)(functools.partial(relay, BEFORE[n]))
 
         live = active(ci)
@@ -317,7 +322,11 @@
                     x = dot_nt(q, k[i:i + n]) * SCALE2 + bias[:, i:i + n]
                     scores[r % 2, :, pl.ds(i, n)] = x
                     for c in range(0, n, D):
-                        top = x[:, c:c + D] if top is None else jnp.maximum(top, x[:, c:c + D])
+                        part = x[:, c:c + D]
+                        if part.shape[1] < D:
+                            fill = jnp.full((PAIR, D - part.shape[1]), NEG, F32)
+                            part = jnp.concatenate([part, fill], axis=1)
+                        top = part if top is None else jnp.maximum(top, part)
                 old = run_max[rows, :]
                 new = jnp.maximum(old, jnp.max(top, axis=1, keepdims=True))
                 run_max[rows, :] = new
@@ -326,8 +335,9 @@
             def weigh(r, new, alpha):
                 rows = pl.ds(r * PAIR, PAIR)
                 for i in range(0, CHUNK, D):
-                    x = scores[r % 2, :, pl.ds(i, D)]
-                    probs[r % 2, :, pl.ds(i, D)] = jnp.exp2(x - new).astype(BF16)
+                    n = min(D, CHUNK - i)
+                    x = scores[r % 2, :, pl.ds(i, n)]
+                    probs[r % 2, :, pl.ds(i, n)] = jnp.exp2(x - new[:, :n]).astype(BF16)
                 out = dot(probs[r % 2], v1)
                 acc[rows, :] = acc[rows, :] * jnp.concatenate([alpha, alpha], axis=1) + out
 
@@ -343,7 +353,7 @@
 
         return carry
 
-    lax.fori_loop(0, SIDE, step, 0)
+    lax.fori_loop(0, CHUNKS, step, 0)
 
     lane_d = lanes(D)
     norm_hi, norm_lo = hi_lo(prefix[:, D:])
@@ -355,20 +365,22 @@
     pick_t = jnp.where((lane_t == 0) | (lane_t == HALF), 1.0, 0.0).astype(BF16)
     v_pick = jnp.concatenate([v_own, pick_t], axis=1)
 
-    def exchange(n, source, target, me, to):
+    def exchange(n, source, target, ring):
+        me = ring[0][1]
+
         def make(j):
             return pltpu.make_async_remote_copy(
                 src_ref=source(j), dst_ref=target.at[me], send_sem=out_sem.at[n, j],
-                recv_sem=in_sem.at[n, me], device_id=to(j), device_id_type=MESH,
+                recv_sem=in_sem.at[n, me], device_id=ring[j][0], device_id_type=MESH,
             )
 
         def gather(own):
             total = own
             for j in NEAR:
-                slot = (me + j) % SIDE
+                slot = ring[j][1]
                 pltpu.make_async_remote_copy(
                     src_ref=source(j), dst_ref=target.at[slot], send_sem=out_sem.at[n, j],
-                    recv_sem=in_sem.at[n, slot], device_id=to(j), device_id_type=MESH,
+                    recv_sem=in_sem.at[n, slot], device_id=ring[j][0], device_id_type=MESH,
                 ).wait_recv()
                 if own is not None:
                     total = total + target[slot].astype(F32)
@@ -385,7 +397,7 @@
         return begin, gather, finished
 
     def tile_exchange(r):
-        return exchange(r, lambda j: parts.at[r, (f + j) % SIDE], got1.at[r], f, f_rank)
+        return exchange(r, lambda j: parts.at[r, f_ring[j][1]], got1.at[r], f_ring)
 
     tiles = [tile_exchange(r) for r in range(TILES)]
 
@@ -450,7 +462,7 @@
         kg_acc[...] += dot(pair_backward_t(kpn[ss, :HALF], kpn[ss, HALF:], d).astype(BF16), k)
         return carry
 
-    lax.fori_loop(0, SIDE, back, 0, unroll=True)
+    lax.fori_loop(0, CHUNKS, back, 0, unroll=True)
     row = lax.broadcasted_iota(jnp.int32, (8, D), 0)
 
     def extra(value):
@@ -464,32 +476,32 @@
     for i in range(SIDE):
         kparts[i] = jnp.concatenate([kg_acc[pl.ds(8 * i, 8), :], tail], axis=0).astype(BF16)
     k_begin, k_one, k_one_end = exchange(
-        4, lambda j: kparts.at[(f + j) % SIDE], kgot1, f, f_rank
+        4, lambda j: kparts.at[f_ring[j][1]], kgot1, f_ring
     )
     k_begin()
     for send in SENDS:
         copy(send).wait_send()
     for r in range(TILES):
         mid[:, pl.ds(r * D, D)] = tiles[r][1](parts[r, f].astype(F32)).astype(BF16)
-    begin, q_two, q_two_end = exchange(5, lambda j: mid, got2, s, s_rank)
+    begin, q_two, q_two_end = exchange(5, lambda j: mid, got2, s_ring)
     begin()
     total = k_one(kparts[f].astype(F32))
     kmid[...] = jnp.concatenate([total[:8], extra(value_of(total))], axis=0).astype(BF16)
-    begin, k_two, k_two_end = exchange(6, lambda j: kmid, kgot2, s, s_rank)
+    begin, k_two, k_two_end = exchange(6, lambda j: kmid, kgot2, s_ring)
     begin()
     for tile in tiles:
         tile[2]()
     k_one_end()
     put.wait()
     full[...] = q_two(mid[...].astype(F32)).astype(BF16)
-    begin, q_three, q_three_end = exchange(7, lambda j: full, got3, f, f_rank)
+    begin, q_three, q_three_end = exchange(7, lambda j: full, got3, f_ring)
     begin()
     total = k_two(kmid[...].astype(F32))
     kfull[...] = total.astype(BF16)
-    begin, k_three, k_three_end = exchange(8, lambda j: kfull, kgot3, f, f_rank)
+    begin, k_three, k_three_end = exchange(8, lambda j: kfull, kgot3, f_ring)
     begin()
     mine[...] = jnp.broadcast_to(value_of(total), (8, D))
-    begin, h_one, h_one_end = exchange(9, lambda j: mine, got_loss, head, h_rank)
+    begin, h_one, h_one_end = exchange(9, lambda j: mine, got_loss, h_ring)
     begin()
     got3[f] = full[...]
     kgot3[f] = kfull[...]
@@ -532,12 +544,12 @@
             pltpu.VMEM((BLOCKS, 2 * T, D), BF16),
             pltpu.VMEM((ROWS, D), BF16),
             pltpu.VMEM((ROWS, D), F32),
-            pltpu.VMEM((SIDE, D, CHUNK), F32),
+            pltpu.VMEM((CHUNKS, D, CHUNK), F32),
             pltpu.VMEM((ROWS, D), F32),
             pltpu.VMEM((ROWS, 2 * D), F32),
             pltpu.VMEM((2, PAIR, CHUNK), F32),
             pltpu.VMEM((2, PAIR, CHUNK), BF16),
-            pltpu.VMEM((SIDE, 1, CHUNK), F32),
+            pltpu.VMEM((CHUNKS, 1, CHUNK), F32),
             pltpu.VMEM((D, 2 * D), F32),
             pltpu.VMEM((D, 2 * D), F32),
             pltpu.VMEM((D, 2 * D), BF16),

time: 79.5 us -> 77.8 us (0.979)
  Pallas kernels: 78.7 us -> 77 us
    pallas_call x1, Pallas kernels: 76.9 us -> 75.1 us  [attend(): pl.pallas_call(main_kernel, out_shape=(jax.ShapeDtypeStruct((T, GROUP * D...]
where the time goes in v6:
time: 77.8 us; the launch traced here: 77.6 us
  Pallas kernels  77 us (99%)
    pallas_call x1, Pallas kernels, attend(): pl.pallas_call(main_kernel, out_shape=(jax.ShapeDtypeStruct((T, GROUP * D...  75.1 us
    pallas_call x1, Pallas kernels, unpack(): pl.pallas_call(unpack_kernel, out_shape=(jax.ShapeDtypeStruct((T, GROUP *...  1.87 us

profile of v6, /device:TPU:1, one launch (start us, length us, event | category | flops | bytes accessed | tf_op | source)
XLA Modules:
  0.0 77.6 jit_solution(12438769417892773380)
XLA Ops:
  0.6 75.1 %attend.1 = (bf16[144,1024]{1,0:T(8,128)(2,1)}, bf16[8,16,512]{2,1,0:T(8,128)(2,1)}, bf16[8,16,128]{2,1,0:T(8,128)(2,1)}, f32[8,128]{1,0:T(8,128)}) custom-call(bf16[144,1024]{1,0:T(8,128)(2,1)} %q_hbm.1, bf16[144,128]{1,0:T(8,128)(2,1)} %k_hbm.1, bf16[144,128]{1,0:T(8,128)(2,1)} %v_hbm.1, bf16[128,512]{1,0:T(8,128)(2,1)} %wq_hbm.1, bf16[64,128]{1,0:T(8,128)(2,1)} %bitcast.3), custom_call_target="tpu_custom_call" | custom-call | tf_op jit(solution)/shard_map/attend/pallas_call | solution.py:533
  75.7 1.9 %unpack.1 = (bf16[144,1024]{1,0:T(8,128)(2,1)}, f32[128,512]{1,0:T(8,128)}, f32[64,128]{1,0:T(8,128)}, f32[1,1]{1,0:T(1,128)}) custom-call(bf16[144,1024]{1,0:T(8,128)(2,1)} %get-tuple-element.12.student_ref, bf16[8,16,512]{2,1,0:T(8,128)(2,1)} %get-tuple-element.13.qg_ref, bf16[8,16,128]{2,1,0:T(8,128)(2,1)} %get-tuple-element.14.kg_ref, ...), custom_call_target="tpu_custom_call" | custom-call | tf_op jit(solution)/shard_map/unpack/pallas_call | solution.py:589

commit v7 on v6

--- a/solution.py
+++ b/solution.py
@@ -481,10 +481,12 @@
     k_begin()
     for send in SENDS:
         copy(send).wait_send()
+    twos = [exchange(10 + i, lambda j, i=i: mid.at[i], got2.at[i], s_ring) for i in range(2)]
+    threes = [exchange(12 + i, lambda j, i=i: full.at[i], got3.at[i], f_ring) for i in range(2)]
     for r in range(TILES):
-        mid[:, pl.ds(r * D, D)] = tiles[r][1](parts[r, f].astype(F32)).astype(BF16)
-    begin, q_two, q_two_end = exchange(5, lambda j: mid, got2, s_ring)
-    begin()
+        mid[r // 2, :, pl.ds(r % 2 * D, D)] = tiles[r][1](parts[r, f].astype(F32)).astype(BF16)
+        if r % 2:
+            twos[r // 2][0]()
     total = k_one(kparts[f].astype(F32))
     kmid[...] = jnp.concatenate([total[:8], extra(value_of(total))], axis=0).astype(BF16)
     begin, k_two, k_two_end = exchange(6, lambda j: kmid, kgot2, s_ring)
@@ -493,9 +495,9 @@
         tile[2]()
     k_one_end()
     put.wait()
-    full[...] = q_two(mid[...].astype(F32)).astype(BF16)
-    begin, q_three, q_three_end = exchange(7, lambda j: full, got3, f_ring)
-    begin()
+    for i in range(2):
+        full[i] = twos[i][1](mid[i].astype(F32)).astype(BF16)
+        threes[i][0]()
     total = k_two(kmid[...].astype(F32))
     kfull[...] = total.astype(BF16)
     begin, k_three, k_three_end = exchange(8, lambda j: kfull, kgot3, f_ring)
@@ -503,22 +505,26 @@
     mine[...] = jnp.broadcast_to(value_of(total), (8, D))
     begin, h_one, h_one_end = exchange(9, lambda j: mine, got_loss, h_ring)
     begin()
-    got3[f] = full[...]
+    for i in range(2):
+        got3[i, f] = full[i]
     kgot3[f] = kfull[...]
-    q_two_end()
+    for two in twos:
+        two[2]()
     k_two_end()
-    q_three(None)
-    qg_ref[...] = got3[...]
+    for i in range(2):
+        threes[i][1](None)
+        qg_ref[i] = got3[i]
     k_three(None)
     kg_ref[...] = kgot3[...]
     loss_ref[...] = h_one(mine[...])
-    for end in (q_three_end, k_three_end, h_one_end):
+    for end in (threes[0][2], threes[1][2], k_three_end, h_one_end):
         end()
 
 
 def unpack_kernel(student_ref, qg_ref, kg_ref, loss_ref, so_ref, qo_ref, ko_ref, lo_ref):
     so_ref[...] = student_ref[...]
-    qo_ref[...] = qg_ref[...].reshape(D, GROUP * HALF).astype(F32)
+    for i in range(2):
+        qo_ref[:, pl.ds(i * 2 * D, 2 * D)] = qg_ref[i].reshape(D, 2 * D).astype(F32)
     for i in range(SIDE):
         ko_ref[pl.ds(8 * i, 8), :] = kg_ref[i].astype(F32)[:8]
     lo_ref[...] = loss_ref[0:1, 0:1] * (1.0 / TOKENS)
@@ -534,7 +540,7 @@
         main_kernel,
         out_shape=(
             jax.ShapeDtypeStruct((T, GROUP * D), BF16),
-            jax.ShapeDtypeStruct((SIDE, 16, GROUP * HALF), BF16),
+            jax.ShapeDtypeStruct((2, SIDE, 16, 2 * D), BF16),
             jax.ShapeDtypeStruct((SIDE, 16, D), BF16),
             jax.ShapeDtypeStruct((8, D), F32),
         ),
@@ -558,7 +564,7 @@
             pltpu.VMEM((HALF, D), F32),
         ]
         + [pltpu.VMEM((TILES,) + all_of + (D,), BF16)] * 2
-        + [pltpu.VMEM(shape + (512,), BF16) for shape in exchanges[2:]]
+        + [pltpu.VMEM((2,) + shape + (2 * D,), BF16) for shape in exchanges[2:]]
         + [pltpu.VMEM(shape + (D,), BF16) for shape in exchanges]
         + [
             pltpu.VMEM((8, D), F32),
@@ -574,8 +580,8 @@
             dma((6,)),
             dma((BLOCKS,)),
             dma((len(SENDS),)),
-            dma((10, SIDE)),
-            dma((10, SIDE)),
+            dma((14, SIDE)),
+            dma((14, SIDE)),
         ],
         compiler_params=pltpu.CompilerParams(
             collective_id=0, has_side_effects=True, vmem_limit_bytes=56 * 1024 * 1024

time: 77.8 us -> 78.3 us (level)
  no operation moved by 1% of the time
where the time goes in v7:
time: 78.3 us; the launch traced here: 78.2 us
  Pallas kernels  77.5 us (99%)
    pallas_call x1, Pallas kernels, attend(): pl.pallas_call(main_kernel, out_shape=(jax.ShapeDtypeStruct((T, GROUP * D...  75.7 us
    pallas_call x1, Pallas kernels, unpack(): pl.pallas_call(unpack_kernel, out_shape=(jax.ShapeDtypeStruct((T, GROUP *...  1.87 us

profile of v7, /device:TPU:1, one launch (start us, length us, event | category | flops | bytes accessed | tf_op | source)
XLA Modules:
  0.0 78.2 jit_solution(2696399872078271281)
XLA Ops:
  0.6 75.7 %attend.1 = (bf16[144,1024]{1,0:T(8,128)(2,1)}, bf16[2,8,16,256]{3,2,1,0:T(8,128)(2,1)}, bf16[8,16,128]{2,1,0:T(8,128)(2,1)}, f32[8,128]{1,0:T(8,128)}) custom-call(bf16[144,1024]{1,0:T(8,128)(2,1)} %q_hbm.1, bf16[144,128]{1,0:T(8,128)(2,1)} %k_hbm.1, bf16[144,128]{1,0:T(8,128)(2,1)} %v_hbm.1, bf16[128,512]{1,0:T(8,128)(2,1)} %wq_hbm.1, bf16[64,128]{1,0:T(8,128)(2,1)} %bitcast.3), custom_call_target="tpu_custom_call" | custom-call | tf_op jit(solution)/shard_map/attend/pallas_call | solution.py:539
  76.3 1.9 %unpack.1 = (bf16[144,1024]{1,0:T(8,128)(2,1)}, f32[128,512]{1,0:T(8,128)}, f32[64,128]{1,0:T(8,128)}, f32[1,1]{1,0:T(1,128)}) custom-call(bf16[144,1024]{1,0:T(8,128)(2,1)} %get-tuple-element.12.student_ref, bf16[2,8,16,256]{3,2,1,0:T(8,128)(2,1)} %get-tuple-element.13.qg_ref, bf16[8,16,128]{2,1,0:T(8,128)(2,1)} %get-tuple-element.14.kg_ref, ...), custom_call_target="tpu_custom_call" | custom-call | tf_op jit(solution)/shard_map/unpack/pallas_call | solution.py:595
